TPU v7x, 256 devices: a whole 4x4x8 slice. The times are simulated.
256 devices in a mesh: gx: 4 (over x), gy: 4 (over y), gz: 16 (over z, core).
Axes of the slice: x: 4, y: 4, z: 8, core: 2. Of those that a mesh axis runs over, the one named last changes fastest.
Arguments:
- solution: float32 [3, 32, 32, 4096], P(None, 'gx', 'gy', 'gz'), may hold values from -6 to 6
- residual: float32 [3, 32, 32, 4096], P(None, 'gx', 'gy', 'gz'), may hold values from -6 to 6
- prev_direction: float32 [3, 32, 32, 4096], P(None, 'gx', 'gy', 'gz'), may hold values from -6 to 6
- prev_image: float32 [3, 32, 32, 4096], P(None, 'gx', 'gy', 'gz'), may hold values from -6 to 6
- prev_rz: float32 [], replicated, may hold values from 4194304 to 16777216
- density_index: int32 [32, 32, 4096], P('gx', 'gy', 'gz'), may hold values from 0 to 15
- stiffness_table: float32 [16], replicated, may hold values from 0.2 to 2
- coarse_inverse: float32 [4, 4, 384, 384], P('gx', 'gy'), may hold values from -0.05 to 5, as said below
Outputs:
- new_solution: float32 [3, 32, 32, 4096], P(None, 'gx', 'gy', 'gz')
- new_residual: float32 [3, 32, 32, 4096], P(None, 'gx', 'gy', 'gz')
- direction: float32 [3, 32, 32, 4096], P(None, 'gx', 'gy', 'gz')
- image: float32 [3, 32, 32, 4096], P(None, 'gx', 'gy', 'gz')
Inputs may be any that keep to these rules, and one draw needn't show every extreme that they name: `coarse_inverse`: each group's matrix is symmetric positive definite.
All inputs are finite; a program needn't handle non-finite values.
Results may differ from a plain program's by a relative error of at most 0.00016.
Values sent between devices are 32-bit elements; how exact they have to be, the bound alone decides.
A program may use at most 128 MiB of HBM per device.

v0:
```python
import math

import jax
import jax.numpy as jnp
from jax import lax
from jax.sharding import PartitionSpec as P

COUPLING = ((1.0, 0.3, 0.3), (0.3, 1.0, 0.3), (0.3, 0.3, 1.0))
DAMPING = 0.6
MASS_SHIFT = 0.1
WEIGHT_BY_KIND = (0.0, 0.1, 0.05, 0.025)


def extended(shard, sides, width):
    for axis, dim in sides:
        count, length = (lax.axis_size(axis), shard.shape[dim])
        up = [(i, (i + 1) % count) for i in range(count - 1)]
        down = [(j, i) for i, j in up]
        last = lax.slice_in_dim(shard, length - width, length, axis=dim)
        leading = lax.slice_in_dim(shard, 0, width, axis=dim)
        before = lax.ppermute(last, axis, up)
        after = lax.ppermute(leading, axis, down)
        shard = jnp.concatenate([before, shard, after], axis=dim)
    return shard


def neighbour_list():
    listing = []
    for step_x in (-1, 0, 1):
        for step_y in (-1, 0, 1):
            for step_z in (-1, 0, 1):
                kind = abs(step_x) + abs(step_y) + abs(step_z)
                if kind > 0:
                    listing.append((step_x, step_y, step_z, 0.5 * WEIGHT_BY_KIND[kind]))
    return listing


def stencil(padded, coeff):
    size_x = padded.shape[1] - 2
    size_y = padded.shape[2] - 2
    size_z = padded.shape[3] - 2
    centre = padded[:, 1:-1, 1:-1, 1:-1]
    coeff_centre = coeff[1:-1, 1:-1, 1:-1]
    total = MASS_SHIFT * coeff_centre * centre
    for step_x, step_y, step_z, weight in neighbour_list():
        other = padded[
            :,
            1 + step_x : 1 + step_x + size_x,
            1 + step_y : 1 + step_y + size_y,
            1 + step_z : 1 + step_z + size_z,
        ]
        other_coeff = coeff[
            1 + step_x : 1 + step_x + size_x,
            1 + step_y : 1 + step_y + size_y,
            1 + step_z : 1 + step_z + size_z,
        ]
        total = total + weight * (coeff_centre + other_coeff) * (centre - other)
    return jnp.stack(
        [
            COUPLING[line][0] * total[0]
            + COUPLING[line][1] * total[1]
            + COUPLING[line][2] * total[2]
            for line in range(3)
        ]
    )


def diagonal_of(coeff):
    size_x = coeff.shape[0] - 2
    size_y = coeff.shape[1] - 2
    size_z = coeff.shape[2] - 2
    coeff_centre = coeff[1:-1, 1:-1, 1:-1]
    total = MASS_SHIFT * coeff_centre
    for step_x, step_y, step_z, weight in neighbour_list():
        other_coeff = coeff[
            1 + step_x : 1 + step_x + size_x,
            1 + step_y : 1 + step_y + size_y,
            1 + step_z : 1 + step_z + size_z,
        ]
        total = total + weight * (coeff_centre + other_coeff)
    return total


def boxed_sum(field, box_x, box_y, box_z):
    shaped = field.reshape(
        3,
        field.shape[1] // box_x,
        box_x,
        field.shape[2] // box_y,
        box_y,
        field.shape[3] // box_z,
        box_z,
    )
    return jnp.sum(shaped, axis=(2, 4, 6))


def coarsen_cells(cells):
    shaped = cells.reshape(cells.shape[0] // 2, 2, cells.shape[1] // 2, 2, cells.shape[2] // 2, 2)
    return jnp.sum(shaped, axis=(1, 3, 5)) * 0.125


def spread_up(field, box_x, box_y, box_z):
    comps, size_x, size_y, size_z = field.shape
    wide = jnp.broadcast_to(
        field[:, :, None, :, None, :, None], (comps, size_x, box_x, size_y, box_y, size_z, box_z)
    )
    return wide.reshape(comps, size_x * box_x, size_y * box_y, size_z * box_z)


def on_device(
    solution,
    residual,
    prev_direction,
    prev_image,
    prev_rz,
    density_index,
    stiffness_table,
    coarse_inverse,
):
    young = jnp.zeros(density_index.shape, jnp.float32)
    for level in range(stiffness_table.shape[0]):
        young = young + jnp.where(density_index == level, stiffness_table[level], 0.0)
    coeff_wide = extended(young, (("gx", 0), ("gy", 1), ("gz", 2)), 2)
    coeff_fine = coeff_wide[1:-1, 1:-1, 1:-1]
    diag_fine = diagonal_of(coeff_fine)
    smooth = DAMPING * residual / diag_fine
    padded = extended(smooth, (("gx", 1), ("gy", 2), ("gz", 3)), 1)
    smooth = smooth + DAMPING * (residual - stencil(padded, coeff_fine)) / diag_fine
    padded = extended(smooth, (("gx", 1), ("gy", 2), ("gz", 3)), 1)
    rest = residual - stencil(padded, coeff_fine)
    coarse_rhs = 0.5 * boxed_sum(rest, 2, 2, 2)
    coeff_mid = extended(coarsen_cells(young), (("gx", 0), ("gy", 1), ("gz", 2)), 1)
    diag_mid = diagonal_of(coeff_mid)
    middle = DAMPING * coarse_rhs / diag_mid
    mid_padded = extended(middle, (("gx", 1), ("gy", 2), ("gz", 3)), 1)
    mid_rest = coarse_rhs - stencil(mid_padded, coeff_mid)
    box_x = middle.shape[1] // 2
    box_y = middle.shape[2] // 2
    box_z = middle.shape[3] // 2
    lowest = boxed_sum(mid_rest, box_x, box_y, box_z) * (1.0 / math.sqrt(box_x * box_y * box_z))
    flat_rhs = lowest.reshape(-1)
    own_rows = flat_rhs.shape[0]
    matrix = coarse_inverse[0, 0]
    offset = lax.axis_index("gz") * own_rows
    whole_rhs = lax.all_gather(flat_rhs, "gz", axis=0, tiled=True)
    own_block = lax.dynamic_slice_in_dim(matrix, offset, own_rows, 0)
    correction = jnp.dot(own_block, whole_rhs, precision=lax.Precision.HIGHEST)
    middle = middle + spread_up(correction.reshape(3, 2, 2, 2), box_x, box_y, box_z)
    mid_padded = extended(middle, (("gx", 1), ("gy", 2), ("gz", 3)), 1)
    middle = middle + DAMPING * (coarse_rhs - stencil(mid_padded, coeff_mid)) / diag_mid
    smooth = smooth + spread_up(middle, 2, 2, 2)
    padded = extended(smooth, (("gx", 1), ("gy", 2), ("gz", 3)), 1)
    smooth = smooth + DAMPING * (residual - stencil(padded, coeff_fine)) / diag_fine
    padded = extended(smooth, (("gx", 1), ("gy", 2), ("gz", 3)), 1)
    precond = smooth + DAMPING * (residual - stencil(padded, coeff_fine)) / diag_fine
    precond_padded = extended(precond, (("gx", 1), ("gy", 2), ("gz", 3)), 1)
    operated = stencil(precond_padded, coeff_fine)
    inner_rz = lax.psum(jnp.sum(residual * precond), ("gx", "gy", "gz"))
    beta = inner_rz / prev_rz
    direction = precond + beta * prev_direction
    image = operated + beta * prev_image
    inner_pq = lax.psum(jnp.sum(direction * image), ("gx", "gy", "gz"))
    alpha = inner_rz / inner_pq
    new_solution = solution + alpha * direction
    new_residual = residual - alpha * image
    return (new_solution, new_residual, direction, image)


def solution(mesh):
    placed = (
        P(None, "gx", "gy", "gz"),
        P(None, "gx", "gy", "gz"),
        P(None, "gx", "gy", "gz"),
        P(None, "gx", "gy", "gz"),
        P(),
        P("gx", "gy", "gz"),
        P(),
        P("gx", "gy", None, None),
    )
    return jax.shard_map(
        on_device,
        mesh=mesh,
        in_specs=placed,
        out_specs=(
            P(None, "gx", "gy", "gz"),
            P(None, "gx", "gy", "gz"),
            P(None, "gx", "gy", "gz"),
            P(None, "gx", "gy", "gz"),
        ),
        check_vma=False,
    )
```

profile of v0, /device:TPU:1, one launch (start us, length us, event | category | flops | bytes accessed | tf_op | source)
XLA Modules:
  0.0 472.4 jit_solution(14138126849225739484)
XLA Ops:
  2.6 11.0 %broadcast_multiply_fusion = (f32[8,8,256]{2,1,0:T(8,128)S(1)}, f32[8,8,256]{2,1,0:T(8,128)S(1)}) fusion(f32[]{:T(128)} %bitcast.15, s32[8,8,256]{2,1,0:T(8,128)} %param.13, f32[]{:T(128)} %bitcast.14, f32[]{:T(128)} %bitcast.13, f32[]{:T(128)} %bitcast.12, f32[]{:T(128)} %bitcast.11, f32[]{:T(128)} %bitcast.10, f32[]{:T(128)} %bitcast.9, f32[]{:T(128)} %bitcast.8, ...), kind=kLoop, calls=%fused_computation.550 | loop fusion | flops 786432 | bytes 196672 | tf_op jit(solution)/shard_map/mul | solution.py:73
  15.0 4.6 collective-permute-start
  19.6 5.6 %reshape.137 = f32[4,2,4,2,128,2]{5,4,3,2,1,0:T(8,128)} reshape(f32[8,8,256]{2,1,0:T(8,128)S(1)} %get-tuple-element.13) | data formatting | bytes 131072 | tf_op jit(solution)/shard_map/reshape | solution.py:98
  36.3 4.1 collective-permute-start.20
  46.8 7.3 %collective-permute-start.5 = (f32[12,12,2]{2,1,0:T(8,128)S(1)}, f32[12,12,2]{2,1,0:T(8,128)S(1)}, u32[]{:S(2)}, u32[]{:S(2)}) collective-permute-start(f32[12,12,2]{2,1,0:T(8,128)S(1)} %get-tuple-element.106), channel_id=1, source_target_pairs={{1,0},{2,1},{3,2},{4,3},{5,4},{6,5},{7,6},{8,7},{9,8},{10,9},{11,1... | collective-permute-start | bytes 3464 | tf_op jit(solution)/shard_map/ppermute | solution.py:22
  59.7 4.0 collective-permute-start.6
  66.0 4.5 collective-permute-start.22
  71.9 4.6 collective-permute-start.8
  84.0 4.4 collective-permute-done.11
  97.5 4.6 collective-permute-start.14
  110.2 4.4 collective-permute-done.17
  116.1 14.0 %reshape.136 = f32[3,4,2,4,2,128,2]{6,5,4,3,2,1,0:T(8,128)} reshape(f32[3,8,8,256]{3,2,1,0:T(8,128)S(1)} %maximum_subtract_fusion.1) | data formatting | bytes 393216 | tf_op jit(solution)/shard_map/reshape | solution.py:85
  130.1 5.5 %reduce_sum.45 = f32[3,4,4,128]{3,2,1,0:T(4,128)S(1)} reduce(f32[3,4,2,4,2,128,2]{6,5,4,3,2,1,0:T(8,128)} %reshape.136, f32[]{:T(128)} %constant.31.clone.1), dimensions={2,4,6}, to_apply=%region_0.1 | reduce | flops 43008 | bytes 221188 | tf_op jit(solution)/shard_map/reduce_sum | solution.py:94
  136.9 4.5 collective-permute-start.24
  143.6 4.6 collective-permute-start.26
  159.3 24.4 %all-reduce = f32[384]{0:T(512)S(1)} all-reduce(f32[384]{0:T(512)S(1)} %dynamic-update-slice), channel_id=1, replica_groups=mesh['gx'=4,'gy'=4,'gz'=16] {'gz'}, use_global_device_ids=true, to_apply=%add | all-reduce | flops 384 | bytes 3072
  186.6 4.5 collective-permute-start.30
  193.3 4.5 collective-permute-start.32
  198.7 5.9 %collective-permute-start.34 = (f32[3,6,6,1]{3,2,1,0:T(8,128)S(1)}, f32[3,6,6,1]{3,2,1,0:T(8,128)S(1)}, u32[]{:S(2)}, u32[]{:S(2)}) collective-permute-start(f32[3,6,6,1]{3,2,1,0:T(8,128)S(1)} %get-tuple-element.114), channel_id=1, source_target_pairs={{0,1},{1,2},{2,3},{3,4},{4,5},{5,6},{6,7},{7,8},{8,9},{9,10},{10,1... | collective-permute-start | bytes 1304 | tf_op jit(solution)/shard_map/ppermute | solution.py:21
  210.7 5.3 %broadcast_in_dim.90 = f32[3,4,2,4,2,128,2]{6,5,4,3,2,1,0:T(8,128)} broadcast(f32[3,4,4,128]{3,2,1,0:T(4,128)S(1)} %divide_add_fusion), dimensions={0,1,3,5} | broadcast | bytes 221184 | tf_op jit(solution)/shard_map/broadcast_in_dim | solution.py:104
  216.0 9.8 %reshape.140 = f32[3,8,8,256]{3,2,1,0:T(8,128)S(1)} reshape(f32[3,4,2,4,2,128,2]{6,5,4,3,2,1,0:T(8,128)} %broadcast_in_dim.90) | data formatting | bytes 393216 | tf_op jit(solution)/shard_map/reshape | solution.py:107
  227.2 4.5 collective-permute-start.36
  234.0 4.5 collective-permute-start.38
  246.9 4.4 collective-permute-done.41
  254.1 4.6 collective-permute-start.42
  261.0 4.6 collective-permute-start.44
  273.5 4.7 collective-permute-done.47
  281.6 4.3 collective-permute-start.48
  288.2 4.6 collective-permute-start.50
  293.4 87.9 %psum.14 = f32[]{:T(128)} all-reduce(f32[]{:T(128)} %get-tuple-element.7), channel_id=1, replica_groups=mesh['gx'=4,'gy'=4,'gz'=16] {'gx','gy','gz'}, use_global_device_ids=true, to_apply=%region_4.5 | all-reduce | flops 1 | bytes 8 | tf_op jit(solution)/shard_map/psum | solution.py:158
  388.0 4.4 collective-permute-done.53
  394.6 75.7 %psum.15 = f32[]{:T(128)} all-reduce(f32[]{:T(128)} %get-tuple-element.4), channel_id=1, replica_groups=mesh['gx'=4,'gy'=4,'gz'=16] {'gx','gy','gz'}, use_global_device_ids=true, to_apply=%region_6.7 | all-reduce | flops 1 | bytes 8 | tf_op jit(solution)/shard_map/psum | solution.py:162
  (200 shorter events, 121.1 us)
Async XLA Ops:
  13.7 26.7 %collective-permute-start.1 = (f32[2,8,256]{2,1,0:T(8,128)S(1)}, f32[2,8,256]{2,1,0:T(8,128)S(1)}, u32[]{:S(2)}, u32[]{:S(2)}) collective-permute-start(f32[2,8,256]{2,1,0:T(8,128)S(1)} %get-tuple-element.119), channel_id=1, source_target_pairs={{64,0},{128,64},{192,128},{65,1},{129,65},{193,129},{66,2},{130,66... | collective-permute-start | bytes 49160 | tf_op jit(solution)/shard_map/ppermute | solution.py:22
  15.0 25.4 %collective-permute-start = (f32[2,8,256]{2,1,0:T(8,128)S(1)}, f32[2,8,256]{2,1,0:T(8,128)S(1)}, u32[]{:S(2)}, u32[]{:S(2)}) collective-permute-start(f32[2,8,256]{2,1,0:T(8,128)S(1)} %get-tuple-element.118), channel_id=1, source_target_pairs={{0,64},{64,128},{128,192},{1,65},{65,129},{129,193},{2,66},{66,130... | collective-permute-start | bytes 49160 | tf_op jit(solution)/shard_map/ppermute | solution.py:21
  27.7 7.3 %collective-permute-start.19 = (f32[1,4,128]{2,1,0:T(4,128)S(1)}, f32[1,4,128]{2,1,0:T(4,128)S(1)}, u32[]{:S(2)}, u32[]{:S(2)}) collective-permute-start(f32[1,4,128]{2,1,0:T(4,128)S(1)} %get-tuple-element.184), channel_id=1, source_target_pairs={{64,0},{128,64},{192,128},{65,1},{129,65},{193,129},{66,2},{130,66... | collective-permute-start | bytes 6152 | tf_op jit(solution)/shard_map/ppermute | solution.py:22
  29.0 6.0 %collective-permute-start.18 = (f32[1,4,128]{2,1,0:T(4,128)S(1)}, f32[1,4,128]{2,1,0:T(4,128)S(1)}, u32[]{:S(2)}, u32[]{:S(2)}) collective-permute-start(f32[1,4,128]{2,1,0:T(4,128)S(1)} %get-tuple-element.183), channel_id=1, source_target_pairs={{0,64},{64,128},{128,192},{1,65},{65,129},{129,193},{2,66},{66,130... | collective-permute-start | bytes 6152 | tf_op jit(solution)/shard_map/ppermute | solution.py:21
  35.0 10.7 %collective-permute-start.21 = (f32[6,1,128]{2,1,0:T(1,128)S(1)}, f32[6,1,128]{2,1,0:T(1,128)S(1)}, u32[]{:S(2)}, u32[]{:S(2)}) collective-permute-start(f32[6,1,128]{2,1,0:T(1,128)S(1)} %get-tuple-element.175), channel_id=1, source_target_pairs={{16,0},{32,16},{48,32},{17,1},{33,17},{49,33},{18,2},{34,18},{50,3... | collective-permute-start | bytes 9224 | tf_op jit(solution)/shard_map/ppermute | solution.py:22
  36.3 9.4 %collective-permute-start.20 = (f32[6,1,128]{2,1,0:T(1,128)S(1)}, f32[6,1,128]{2,1,0:T(1,128)S(1)}, u32[]{:S(2)}, u32[]{:S(2)}) collective-permute-start(f32[6,1,128]{2,1,0:T(1,128)S(1)} %get-tuple-element.174), channel_id=1, source_target_pairs={{0,16},{16,32},{32,48},{1,17},{17,33},{33,49},{2,18},{18,34},{34,5... | collective-permute-start | bytes 9224 | tf_op jit(solution)/shard_map/ppermute | solution.py:21
  46.8 9.4 %collective-permute-start.5 = (f32[12,12,2]{2,1,0:T(8,128)S(1)}, f32[12,12,2]{2,1,0:T(8,128)S(1)}, u32[]{:S(2)}, u32[]{:S(2)}) collective-permute-start(f32[12,12,2]{2,1,0:T(8,128)S(1)} %get-tuple-element.106), channel_id=1, source_target_pairs={{1,0},{2,1},{3,2},{4,3},{5,4},{6,5},{7,6},{8,7},{9,8},{10,9},{11,1... | collective-permute-start | bytes 3464 | tf_op jit(solution)/shard_map/ppermute | solution.py:22
  58.4 12.2 %collective-permute-start.7 = (f32[3,1,8,256]{3,2,1,0:T(8,128)S(1)}, f32[3,1,8,256]{3,2,1,0:T(8,128)S(1)}, u32[]{:S(2)}, u32[]{:S(2)}) collective-permute-start(f32[3,1,8,256]{3,2,1,0:T(8,128)S(1)} %get-tuple-element.105), channel_id=1, source_target_pairs={{64,0},{128,64},{192,128},{65,1},{129,65},{193,129},{66,2},{130,66... | collective-permute-start | bytes 73736 | tf_op jit(solution)/shard_map/ppermute | solution.py:22
  59.7 10.9 %collective-permute-start.6 = (f32[3,1,8,256]{3,2,1,0:T(8,128)S(1)}, f32[3,1,8,256]{3,2,1,0:T(8,128)S(1)}, u32[]{:S(2)}, u32[]{:S(2)}) collective-permute-start(f32[3,1,8,256]{3,2,1,0:T(8,128)S(1)} %get-tuple-element.104), channel_id=1, source_target_pairs={{0,64},{64,128},{128,192},{1,65},{65,129},{129,193},{2,66},{66,130... | collective-permute-start | bytes 73736 | tf_op jit(solution)/shard_map/ppermute | solution.py:21
  63.7 31.5 %collective-permute-start.23 = (f32[6,6,1]{2,1,0:T(8,128)S(1)}, f32[6,6,1]{2,1,0:T(8,128)S(1)}, u32[]{:S(2)}, u32[]{:S(2)}) collective-permute-start(f32[6,6,1]{2,1,0:T(8,128)S(1)} %get-tuple-element.168), channel_id=1, source_target_pairs={{1,0},{2,1},{3,2},{4,3},{5,4},{6,5},{7,6},{8,7},{9,8},{10,9},{11,1... | collective-permute-start | bytes 440 | tf_op jit(solution)/shard_map/ppermute | solution.py:22
  66.0 29.3 %collective-permute-start.22 = (f32[6,6,1]{2,1,0:T(8,128)S(1)}, f32[6,6,1]{2,1,0:T(8,128)S(1)}, u32[]{:S(2)}, u32[]{:S(2)}) collective-permute-start(f32[6,6,1]{2,1,0:T(8,128)S(1)} %get-tuple-element.169), channel_id=1, source_target_pairs={{0,1},{1,2},{2,3},{3,4},{4,5},{5,6},{6,7},{7,8},{8,9},{9,10},{10,1... | collective-permute-start | bytes 440 | tf_op jit(solution)/shard_map/ppermute | solution.py:21
  70.6 5.9 %collective-permute-start.9 = (f32[3,10,1,256]{3,2,1,0:T(1,128)S(1)}, f32[3,10,1,256]{3,2,1,0:T(1,128)S(1)}, u32[]{:S(2)}, u32[]{:S(2)}) collective-permute-start(f32[3,10,1,256]{3,2,1,0:T(1,128)S(1)} %get-tuple-element.80), channel_id=1, source_target_pairs={{16,0},{32,16},{48,32},{17,1},{33,17},{49,33},{18,2},{34,18},{50,3... | collective-permute-start | bytes 92168 | tf_op jit(solution)/shard_map/ppermute | solution.py:22
  77.7 6.4 %collective-permute-start.10 = (f32[3,10,10,1]{3,2,1,0:T(8,128)S(1)}, f32[3,10,10,1]{3,2,1,0:T(8,128)S(1)}, u32[]{:S(2)}, u32[]{:S(2)}) collective-permute-start(f32[3,10,10,1]{3,2,1,0:T(8,128)S(1)} %get-tuple-element.49), channel_id=1, source_target_pairs={{0,1},{1,2},{2,3},{3,4},{4,5},{5,6},{6,7},{7,8},{8,9},{9,10},{10,1... | collective-permute-start | bytes 3608 | tf_op jit(solution)/shard_map/ppermute | solution.py:21
  80.9 7.5 %collective-permute-start.11 = (f32[3,10,10,1]{3,2,1,0:T(8,128)S(1)}, f32[3,10,10,1]{3,2,1,0:T(8,128)S(1)}, u32[]{:S(2)}, u32[]{:S(2)}) collective-permute-start(f32[3,10,10,1]{3,2,1,0:T(8,128)S(1)} %get-tuple-element.50), channel_id=1, source_target_pairs={{1,0},{2,1},{3,2},{4,3},{5,4},{6,5},{7,6},{8,7},{9,8},{10,9},{11,1... | collective-permute-start | bytes 3608 | tf_op jit(solution)/shard_map/ppermute | solution.py:22
  96.2 6.0 %collective-permute-start.15 = (f32[3,10,1,256]{3,2,1,0:T(1,128)S(1)}, f32[3,10,1,256]{3,2,1,0:T(1,128)S(1)}, u32[]{:S(2)}, u32[]{:S(2)}) collective-permute-start(f32[3,10,1,256]{3,2,1,0:T(1,128)S(1)} %get-tuple-element.76), channel_id=1, source_target_pairs={{16,0},{32,16},{48,32},{17,1},{33,17},{49,33},{18,2},{34,18},{50,3... | collective-permute-start | bytes 92168 | tf_op jit(solution)/shard_map/ppermute | solution.py:22
  103.3 6.9 %collective-permute-start.16 = (f32[3,10,10,1]{3,2,1,0:T(8,128)S(1)}, f32[3,10,10,1]{3,2,1,0:T(8,128)S(1)}, u32[]{:S(2)}, u32[]{:S(2)}) collective-permute-start(f32[3,10,10,1]{3,2,1,0:T(8,128)S(1)} %get-tuple-element.47), channel_id=1, source_target_pairs={{0,1},{1,2},{2,3},{3,4},{4,5},{5,6},{6,7},{7,8},{8,9},{9,10},{10,1... | collective-permute-start | bytes 3608 | tf_op jit(solution)/shard_map/ppermute | solution.py:21
  107.1 7.5 %collective-permute-start.17 = (f32[3,10,10,1]{3,2,1,0:T(8,128)S(1)}, f32[3,10,10,1]{3,2,1,0:T(8,128)S(1)}, u32[]{:S(2)}, u32[]{:S(2)}) collective-permute-start(f32[3,10,10,1]{3,2,1,0:T(8,128)S(1)} %get-tuple-element.48), channel_id=1, source_target_pairs={{1,0},{2,1},{3,2},{4,3},{5,4},{6,5},{7,6},{8,7},{9,8},{10,9},{11,1... | collective-permute-start | bytes 3608 | tf_op jit(solution)/shard_map/ppermute | solution.py:22
  135.6 5.9 %collective-permute-start.25 = (f32[3,1,4,128]{3,2,1,0:T(4,128)S(1)}, f32[3,1,4,128]{3,2,1,0:T(4,128)S(1)}, u32[]{:S(2)}, u32[]{:S(2)}) collective-permute-start(f32[3,1,4,128]{3,2,1,0:T(4,128)S(1)} %get-tuple-element.165), channel_id=1, source_target_pairs={{64,0},{128,64},{192,128},{65,1},{129,65},{193,129},{66,2},{130,66... | collective-permute-start | bytes 18440 | tf_op jit(solution)/shard_map/ppermute | solution.py:22
  142.3 6.1 %collective-permute-start.27 = (f32[3,6,1,128]{3,2,1,0:T(1,128)S(1)}, f32[3,6,1,128]{3,2,1,0:T(1,128)S(1)}, u32[]{:S(2)}, u32[]{:S(2)}) collective-permute-start(f32[3,6,1,128]{3,2,1,0:T(1,128)S(1)} %get-tuple-element.149), channel_id=1, source_target_pairs={{16,0},{32,16},{48,32},{17,1},{33,17},{49,33},{18,2},{34,18},{50,3... | collective-permute-start | bytes 27656 | tf_op jit(solution)/shard_map/ppermute | solution.py:22
  192.0 5.8 %collective-permute-start.33 = (f32[3,6,1,128]{3,2,1,0:T(1,128)S(1)}, f32[3,6,1,128]{3,2,1,0:T(1,128)S(1)}, u32[]{:S(2)}, u32[]{:S(2)}) collective-permute-start(f32[3,6,1,128]{3,2,1,0:T(1,128)S(1)} %get-tuple-element.145), channel_id=1, source_target_pairs={{16,0},{32,16},{48,32},{17,1},{33,17},{49,33},{18,2},{34,18},{50,3... | collective-permute-start | bytes 27656 | tf_op jit(solution)/shard_map/ppermute | solution.py:22
  198.7 7.9 %collective-permute-start.34 = (f32[3,6,6,1]{3,2,1,0:T(8,128)S(1)}, f32[3,6,6,1]{3,2,1,0:T(8,128)S(1)}, u32[]{:S(2)}, u32[]{:S(2)}) collective-permute-start(f32[3,6,6,1]{3,2,1,0:T(8,128)S(1)} %get-tuple-element.114), channel_id=1, source_target_pairs={{0,1},{1,2},{2,3},{3,4},{4,5},{5,6},{6,7},{7,8},{8,9},{9,10},{10,1... | collective-permute-start | bytes 1304 | tf_op jit(solution)/shard_map/ppermute | solution.py:21
  225.9 5.8 %collective-permute-start.37 = (f32[3,1,8,256]{3,2,1,0:T(8,128)S(1)}, f32[3,1,8,256]{3,2,1,0:T(8,128)S(1)}, u32[]{:S(2)}, u32[]{:S(2)}) collective-permute-start(f32[3,1,8,256]{3,2,1,0:T(8,128)S(1)} %get-tuple-element.95), channel_id=1, source_target_pairs={{64,0},{128,64},{192,128},{65,1},{129,65},{193,129},{66,2},{130,66... | collective-permute-start | bytes 73736 | tf_op jit(solution)/shard_map/ppermute | solution.py:22
  232.7 5.9 %collective-permute-start.39 = (f32[3,10,1,256]{3,2,1,0:T(1,128)S(1)}, f32[3,10,1,256]{3,2,1,0:T(1,128)S(1)}, u32[]{:S(2)}, u32[]{:S(2)}) collective-permute-start(f32[3,10,1,256]{3,2,1,0:T(1,128)S(1)} %get-tuple-element.72), channel_id=1, source_target_pairs={{16,0},{32,16},{48,32},{17,1},{33,17},{49,33},{18,2},{34,18},{50,3... | collective-permute-start | bytes 92168 | tf_op jit(solution)/shard_map/ppermute | solution.py:22
  239.8 7.1 %collective-permute-start.40 = (f32[3,10,10,1]{3,2,1,0:T(8,128)S(1)}, f32[3,10,10,1]{3,2,1,0:T(8,128)S(1)}, u32[]{:S(2)}, u32[]{:S(2)}) collective-permute-start(f32[3,10,10,1]{3,2,1,0:T(8,128)S(1)} %get-tuple-element.45), channel_id=1, source_target_pairs={{0,1},{1,2},{2,3},{3,4},{4,5},{5,6},{6,7},{7,8},{8,9},{9,10},{10,1... | collective-permute-start | bytes 3608 | tf_op jit(solution)/shard_map/ppermute | solution.py:21
  243.8 7.5 %collective-permute-start.41 = (f32[3,10,10,1]{3,2,1,0:T(8,128)S(1)}, f32[3,10,10,1]{3,2,1,0:T(8,128)S(1)}, u32[]{:S(2)}, u32[]{:S(2)}) collective-permute-start(f32[3,10,10,1]{3,2,1,0:T(8,128)S(1)} %get-tuple-element.46), channel_id=1, source_target_pairs={{1,0},{2,1},{3,2},{4,3},{5,4},{6,5},{7,6},{8,7},{9,8},{10,9},{11,1... | collective-permute-start | bytes 3608 | tf_op jit(solution)/shard_map/ppermute | solution.py:22
  252.8 5.9 %collective-permute-start.43 = (f32[3,1,8,256]{3,2,1,0:T(8,128)S(1)}, f32[3,1,8,256]{3,2,1,0:T(8,128)S(1)}, u32[]{:S(2)}, u32[]{:S(2)}) collective-permute-start(f32[3,1,8,256]{3,2,1,0:T(8,128)S(1)} %get-tuple-element.90), channel_id=1, source_target_pairs={{64,0},{128,64},{192,128},{65,1},{129,65},{193,129},{66,2},{130,66... | collective-permute-start | bytes 73736 | tf_op jit(solution)/shard_map/ppermute | solution.py:22
  259.7 5.9 %collective-permute-start.45 = (f32[3,10,1,256]{3,2,1,0:T(1,128)S(1)}, f32[3,10,1,256]{3,2,1,0:T(1,128)S(1)}, u32[]{:S(2)}, u32[]{:S(2)}) collective-permute-start(f32[3,10,1,256]{3,2,1,0:T(1,128)S(1)} %get-tuple-element.68), channel_id=1, source_target_pairs={{16,0},{32,16},{48,32},{17,1},{33,17},{49,33},{18,2},{34,18},{50,3... | collective-permute-start | bytes 92168 | tf_op jit(solution)/shard_map/ppermute | solution.py:22
  266.8 6.7 %collective-permute-start.46 = (f32[3,10,10,1]{3,2,1,0:T(8,128)S(1)}, f32[3,10,10,1]{3,2,1,0:T(8,128)S(1)}, u32[]{:S(2)}, u32[]{:S(2)}) collective-permute-start(f32[3,10,10,1]{3,2,1,0:T(8,128)S(1)} %get-tuple-element.43), channel_id=1, source_target_pairs={{0,1},{1,2},{2,3},{3,4},{4,5},{5,6},{6,7},{7,8},{8,9},{9,10},{10,1... | collective-permute-start | bytes 3608 | tf_op jit(solution)/shard_map/ppermute | solution.py:21
  270.4 7.8 %collective-permute-start.47 = (f32[3,10,10,1]{3,2,1,0:T(8,128)S(1)}, f32[3,10,10,1]{3,2,1,0:T(8,128)S(1)}, u32[]{:S(2)}, u32[]{:S(2)}) collective-permute-start(f32[3,10,10,1]{3,2,1,0:T(8,128)S(1)} %get-tuple-element.44), channel_id=1, source_target_pairs={{1,0},{2,1},{3,2},{4,3},{5,4},{6,5},{7,6},{8,7},{9,8},{10,9},{11,1... | collective-permute-start | bytes 3608 | tf_op jit(solution)/shard_map/ppermute | solution.py:22
  286.9 95.1 %collective-permute-start.51 = (f32[3,10,1,256]{3,2,1,0:T(1,128)S(1)}, f32[3,10,1,256]{3,2,1,0:T(1,128)S(1)}, u32[]{:S(2)}, u32[]{:S(2)}) collective-permute-start(f32[3,10,1,256]{3,2,1,0:T(1,128)S(1)} %get-tuple-element.64), channel_id=1, source_target_pairs={{16,0},{32,16},{48,32},{17,1},{33,17},{49,33},{18,2},{34,18},{50,3... | collective-permute-start | bytes 92168 | tf_op jit(solution)/shard_map/ppermute | solution.py:22
  288.2 93.8 %collective-permute-start.50 = (f32[3,10,1,256]{3,2,1,0:T(1,128)S(1)}, f32[3,10,1,256]{3,2,1,0:T(1,128)S(1)}, u32[]{:S(2)}, u32[]{:S(2)}) collective-permute-start(f32[3,10,1,256]{3,2,1,0:T(1,128)S(1)} %get-tuple-element.63), channel_id=1, source_target_pairs={{0,16},{16,32},{32,48},{1,17},{17,33},{33,49},{2,18},{18,34},{34,5... | collective-permute-start | bytes 92168 | tf_op jit(solution)/shard_map/ppermute | solution.py:21
  384.9 7.5 %collective-permute-start.53 = (f32[3,10,10,1]{3,2,1,0:T(8,128)S(1)}, f32[3,10,10,1]{3,2,1,0:T(8,128)S(1)}, u32[]{:S(2)}, u32[]{:S(2)}) collective-permute-start(f32[3,10,10,1]{3,2,1,0:T(8,128)S(1)} %get-tuple-element.42), channel_id=1, source_target_pairs={{1,0},{2,1},{3,2},{4,3},{5,4},{6,5},{7,6},{8,7},{9,8},{10,9},{11,1... | collective-permute-start | bytes 3608 | tf_op jit(solution)/shard_map/ppermute | solution.py:22
  (29 other events, 817.1 us)
where the time goes:
time: 475 us; the launch traced here: 472 us
  blocking collectives  188 us (40%)
  starting transfers between devices  158 us (33%)
  waiting for transfers between devices  47.4 us (10%)
  local copies, waits for them, and re-layouts  39.9 us (8%)
  other arithmetic  32.2 us (7%)
  between operations  5.17 us (1%)
    ppermute x27, starting transfers between devices, extended(): before = lax.ppermute(last, axis, up)  112 us
    psum x1, blocking collectives, on_device(): inner_rz = lax.psum(jnp.sum(residual * precond), ('gx', 'gy', 'gz'))  87.9 us
    psum x1, blocking collectives, on_device(): inner_pq = lax.psum(jnp.sum(direction * image), ('gx', 'gy', 'gz'))  75.7 us
    ppermute x27, starting transfers between devices, extended(): after = lax.ppermute(leading, axis, down)  46.4 us
    ppermute x27, waiting for transfers between devices, extended(): after = lax.ppermute(leading, axis, down)  29.6 us
    unnamed x1, blocking collectives  24.4 us
    ppermute x27, waiting for transfers between devices, extended(): before = lax.ppermute(last, axis, up)  17.8 us
    reshape x1, local copies, waits for them, and re-layouts, boxed_sum(): field.reshape(3, field.shape[1] // box_x, box_x, field.shape[2] // box_y,...  14 us
  transfers between devices with their start and end apart: 54, of which 27 were waited for; matrix products, arithmetic and copies ran while one was open for 3% of the time, Pallas kernels for 0%

commit v1 on v0

v1 whole, which is shorter than its diff:
```python
import functools
import itertools
import math

import jax
import jax.numpy as jnp
from jax import lax
from jax.experimental import pallas as pl
from jax.experimental.pallas import tpu as pltpu
from jax.sharding import PartitionSpec as P


MESH = pl.DeviceIdType.MESH
AXES = ("gx", "gy", "gz")
F32 = jnp.float32
HIGH = lax.Precision.HIGHEST
DAMP = 0.6
EIGHTIETH = 0.0125
SMALL = (-1, 0, 1)


def iota(shape, dim):
    return lax.broadcasted_iota(jnp.int32, shape, dim)


def smooth_rows_lanes(v):
    rows, lanes = v.shape
    v = (v + v) + (pltpu.roll(v, 1, 0) + pltpu.roll(v, rows - 1, 0))
    return (v + v) + (pltpu.roll(v, 1, 1) + pltpu.roll(v, lanes - 1, 1))


def three(low, mid, high):
    return (mid + mid) + (low + high)


def operate(field, coeff, centre, at):
    e_low, e_mid, e_high = coeff(at - 1), coeff(at), coeff(at + 1)
    own = centre(at)
    parts = []
    for c in range(3):
        low, mid, high = field(c, at - 1), field(c, at), field(c, at + 1)
        plain = smooth_rows_lanes(three(low, mid, high))
        scaled = smooth_rows_lanes(three(e_low * low, e_mid * mid, e_high * high))
        parts.append(own * mid - EIGHTIETH * (e_mid * plain + scaled))
    shared = 0.3 * (parts[0] + parts[1] + parts[2])
    return [0.7 * part + shared for part in parts]


def centre_terms(low, mid, high):
    wide = EIGHTIETH * smooth_rows_lanes(three(low, mid, high))
    inverse = jnp.where(mid > 0.0, DAMP / (0.7 * mid + wide), 0.0)
    return 0.9 * mid + wide, inverse


def dot(a, b):
    return jnp.dot(a, b, precision=HIGH, preferred_element_type=F32)


def kernel(
    ng,
    res_hbm, dir_hbm, img_hbm, dens_hbm, inv_hbm, table, prev_rz,
    p_out, ap_out, ab_out,
    dens, res, ewide, emask, e16, cen, dinv, s_a, s_b, pdir, pimg,
    spack, srecv, ysum, km, cen1, dinv1, m_a, tlow,
    mpack, mrecv, wd, cenw, dinvw, m_b, m_c, u8,
    rz_mat, gsend, grecv, rows, vown, vrecv,
    dsend, drecv, esend, erecv,
    lsem, sems, recs,
):
    gx, gy, gz = (lax.axis_index(a) for a in AXES)
    me = (gx, gy, gz)

    def device(d):
        return tuple(lax.rem(me[i] + (d[i] % ng[i]), ng[i]) for i in range(3))

    near = [d for d in itertools.product(SMALL, repeat=3) if d != (0, 0, 0)]
    flat = [d for d in near if d[2] == 0]
    column = [(0, 0, k) for k in range(1, ng[2])]
    layer = [(i, j, 0) for i in range(ng[0]) for j in range(ng[1]) if (i, j) != (0, 0)]
    partners = []
    for d in near + column + layer:
        d = tuple(d[i] % ng[i] for i in range(3))
        if d not in partners:
            partners.append(d)

    barrier = pltpu.get_barrier_semaphore()
    for d in partners:
        pl.semaphore_signal(barrier, inc=1, device_id=device(d), device_id_type=MESH)
    loads = [
        pltpu.make_async_copy(dens_hbm, dens, lsem.at[0]),
        pltpu.make_async_copy(res_hbm, res.at[:, 4:12, 0:8, 0:256], lsem.at[1]),
        pltpu.make_async_copy(dir_hbm, pdir, lsem.at[2]),
        pltpu.make_async_copy(img_hbm, pimg, lsem.at[3]),
    ]
    for b in range(3):
        block = jnp.clip(gz + (b - 1), 0, ng[2] - 1)
        start = pl.multiple_of(block * 24, 8)
        loads.append(
            pltpu.make_async_copy(
                inv_hbm.at[0, 0, pl.ds(start, 24), :], rows.at[24 * b : 24 * b + 24, :], lsem.at[4 + b]
            )
        )
    for copy in loads:
        copy.start()
    rows[72:128, :] = jnp.zeros((56, rows.shape[1]), F32)
    loads[0].wait()

    @pl.loop(0, 8)
    def _(x):
        index = dens[x]
        young = jnp.full(index.shape, table[0], F32)
        for level in range(1, table.shape[0]):
            young = jnp.where(index == level, table[level], young)
        ewide[5 + x, 8:16, 0:256] = young

    loads[1].wait()

    lane8 = iota((8, 128), 1)
    row8 = iota((8, 128), 0)
    slot8 = lane8 // 8

    def fine_tile(f, x, at):
        if f < 3:
            return res[f, 4 + x, 0:8, at : at + 128]
        return ewide[5 + x, 8:16, at : at + 128]

    for side, (at, extra) in enumerate(((0, 0), (128, 8))):
        for t in range(2):
            def pack_one(x, total, t=t, at=at, extra=extra):
                for k in range(2):
                    s = k * 8 + x
                    moved = pltpu.roll(fine_tile(2 * t + k, x, at), lax.rem(8 * s + extra, 128), 1)
                    total = jnp.where(slot8 == s, moved, total)
                return total

            spack[side, t] = lax.fori_loop(0, 8, pack_one, jnp.zeros((8, 128), F32))

    pl.semaphore_wait(barrier, len(partners))

    started = []
    counter = [0]

    def send(src, dst, d):
        k = counter[0]
        counter[0] = k + 1
        copy = pltpu.make_async_remote_copy(
            src_ref=src, dst_ref=dst, send_sem=sems.at[k], recv_sem=recs.at[k],
            device_id=device(d), device_id_type=MESH,
        )
        copy.start()
        started.append(copy)
        return copy

    round_a = []
    pick = {
        -1: (slice(4, 8), slice(12, 16)), 0: (slice(4, 12), slice(4, 12)), 1: (slice(8, 12), slice(0, 4)),
    }
    pick_row = {-1: (slice(0, 4), slice(8, 12)), 0: (slice(0, 8), slice(0, 8)), 1: (slice(4, 8), slice(12, 16))}
    pick_e = {
        -1: (slice(5, 10), slice(13, 18)), 0: (slice(5, 13), slice(5, 13)), 1: (slice(8, 13), slice(0, 5)),
    }
    pick_e_row = {-1: slice(16, 24), 0: slice(8, 16), 1: slice(0, 8)}
    main = slice(0, 256)
    for d in flat:
        src = res.at[:, pick[d[0]][0], pick_row[d[1]][0], main]
        dst = res.at[:, pick[d[0]][1], pick_row[d[1]][1], main]
        round_a.append(send(src, dst, d))
    for d in flat:
        src = ewide.at[pick_e[d[0]][0], slice(8, 16), main]
        dst = ewide.at[pick_e[d[0]][1], pick_e_row[d[1]], main]
        round_a.append(send(src, dst, d))
    for d in near:
        if d[2] != 0:
            side = 0 if d[2] < 0 else 1
            round_a.append(send(spack.at[side], srecv.at[side, 1 - d[0], 1 - d[1]], d))

    lane_of = iota((384, 256), 0)
    target = jnp.where(lane_of < 320, lane_of // 2, lane_of // 2 + 64)
    rz_mat[...] = jnp.where(iota((384, 256), 1) == target, 1.0, 0.0)

    for copy in round_a:
        copy.wait_recv()

    def rim(right, left, s):
        to_right = pltpu.roll(right, lax.rem(256 - 8 * s, 128), 1)
        to_left = pltpu.roll(left, lax.rem(256 - 8 * s - 8, 128), 1)
        return jnp.where(lane8 < 64, to_right, to_left)

    rim_lanes = slice(256, 384)
    for ox, first, count, base in ((-1, 4, 4, 0), (0, 0, 8, 4), (1, 0, 4, 12)):
        for t in range(2):
            tiles = []
            for side in range(2):
                tiles.append(srecv[side, ox + 1, 1, t] if True else None)
            mixed = [
                jnp.where(row8 < 4, srecv[side, ox + 1, 2, t], srecv[side, ox + 1, 0, t]) for side in range(2)
            ]

            @pl.loop(0, count)
            def _(i, t=t, first=first, base=base, tiles=tiles, mixed=mixed):
                for k in range(2):
                    if 2 * t + k < 3:
                        s = k * 8 + first + i
                        res[2 * t + k, base + i, 0:8, rim_lanes] = rim(tiles[0], tiles[1], s)
                        res[2 * t + k, base + i, 8:16, rim_lanes] = rim(mixed[0], mixed[1], s)

    for ox, first, count, base in ((-1, 3, 5, 0), (0, 0, 8, 5), (1, 0, 5, 13)):
        tiles = [[srecv[side, ox + 1, oy, 1] for side in range(2)] for oy in range(3)]

        @pl.loop(0, count)
        def _(i, first=first, base=base, tiles=tiles):
            for oy in range(3):
                ewide[base + i, 8 * oy : 8 * oy + 8, rim_lanes] = rim(tiles[oy][0], tiles[oy][1], 8 + first + i)

    row24 = iota((24, 384), 0)
    lane24 = iota((24, 384), 1)
    y_at = gy * 8 + row24 - 8
    z_at = gz * 256 + jnp.where(lane24 < 320, lane24, lane24 - 384)
    inside = (y_at >= 0) & (y_at < 8 * ng[1]) & (z_at >= 0) & (z_at < 256 * ng[2])
    inside = jnp.where(inside & ((lane24 < 264) | (lane24 >= 376)), 1, 0)

    @pl.loop(0, 18)
    def _(x):
        x_at = gx * 8 + x - 5
        x_in = jnp.where((x_at >= 0) & (x_at < 8 * ng[0]), 1, 0)
        emask[x] = jnp.where(inside * x_in > 0, ewide[x], 0.0)

    upper = iota((8, 384), 0) < 4

    @pl.loop(0, 16)
    def _(x):
        mid = emask[x + 1]
        own, inverse = centre_terms(emask[x], mid, emask[x + 2])
        for value, out in ((mid, e16), (own, cen), (inverse, dinv)):
            out[x, 0:8, :] = value[8:16]
            out[x, 8:16, :] = jnp.where(upper, value[16:24], value[0:8])
        for c in range(3):
            s_a[c, x] = dinv[x] * res[c, x]

    def fine(ref):
        return functools.partial(
            operate, lambda c, x: ref[c, x], lambda x: e16[x], lambda x: cen[x]
        )

    def sweep(source, out, start, stop):
        @pl.loop(start, stop)
        def _(x):
            image = fine(source)(x)
            for c in range(3):
                out[c, x] = source[c, x] + dinv[x] * (res[c, x] - image[c])

    sweep(s_a, s_b, 1, 15)

    def put_tiles(ref, f, k, value):
        for t in range(3):
            ref[f, k, t] = value[:, 128 * t : 128 * t + 128]

    @pl.loop(0, 6)
    def _(k):
        x = 2 * k + 2
        first, second = fine(s_b)(x), fine(s_b)(x + 1)
        for c in range(3):
            both = (res[c, x] - first[c]) + (res[c, x + 1] - second[c])
            put_tiles(ysum, c, k + 1, both + pltpu.roll(both, 15, 0))

    @pl.loop(0, 8)
    def _(k):
        both = e16[2 * k] + e16[2 * k + 1]
        put_tiles(ysum, 3, k, both + pltpu.roll(both, 15, 0))

    for c in range(3):
        for k in (0, 7):
            ysum[c, k] = jnp.zeros((3, 16, 128), F32)

    total = None
    for t in range(3):
        left = ysum[:, :, t, pl.ds(0, 8, stride=2), :].reshape(256, 128)
        part = dot(left, rz_mat[128 * t : 128 * t + 128, :])
        total = part if total is None else total + part
    total = total.reshape(4, 8, 8, 256)
    km[0:3] = 0.5 * total[0:3]
    km[3] = 0.125 * total[3]

    @pl.loop(1, 7)
    def _(k):
        own, inverse = centre_terms(km[3, k - 1], km[3, k], km[3, k + 1])
        cen1[k] = own
        dinv1[k] = inverse
        for c in range(3):
            m_a[c, k] = inverse * km[c, k]

    @pl.loop(0, 2)
    def _(b):
        x = 2 * b + 2
        apply = functools.partial(
            operate, lambda c, k: m_a[c, k], lambda k: km[3, k], lambda k: cen1[k]
        )
        first, second = apply(x), apply(x + 1)
        for c in range(3):
            both = (km[c, x] - first[c]) + (km[c, x + 1] - second[c])
            tlow[2 * c + b] = both[:, 0:128]

    place = iota((128, 384), 1) - 24 * gz
    halves = jnp.where((place & 1) == iota((128, 384), 0) // 64, 1.0 / 16.0, 0.0)
    spread = dot(tlow[...].reshape(48, 128), halves)
    place = iota((48, 384), 1) - 24 * gz
    row48 = iota((48, 384), 0)
    keep = (place >= 0) & (place < 24) & ((place // 4) == (row48 // 8))
    keep = keep & ((row48 % 8) // 2 == (place // 2) % 2) & (row48 % 8 < 4)
    own_g = jnp.sum(jnp.where(keep, spread, 0.0), axis=0, keepdims=True)
    gsend[...] = own_g
    round_b = [send(gsend, grecv.at[k], d) for k, d in enumerate(column)]

    low = iota((8, 128), 0) < 4
    for side, (at, extra) in enumerate(((0, 0), (0, 8))):
        total = jnp.zeros((8, 128), F32)
        for f in range(4):
            for x in range(4):
                s = 4 * f + x
                moved = pltpu.roll(km[f, 2 + x, :, 0:128], (8 * s + extra) % 128, 1)
                total = jnp.where(slot8 == s, moved, total)
        mpack[side] = jnp.where(low, total, pltpu.roll(total, 4, 0))
    round_c = []
    mid_x = {-1: slice(8, 12), 0: slice(4, 8), 1: slice(0, 4)}
    mid_row = {-1: slice(4, 8), 0: slice(0, 4), 1: slice(12, 16)}
    block = km.at[:, 2:6, 0:4, 0:128]
    for d in flat:
        round_c.append(send(block, wd.at[:, mid_x[d[0]], mid_row[d[1]], 0:128], d))
    for d in near:
        if d[2] != 0:
            side = 0 if d[2] < 0 else 1
            round_c.append(send(mpack.at[side], mrecv.at[side, 1 - d[0], 1 - d[1]], d))
    for f in range(4):
        wd[f, 4:8, 0:4, 0:128] = km[f, 2:6, 0:4, 0:128]
        wd[f, :, 8:12, 0:128] = jnp.zeros((12, 4, 128), F32)
    for copy in round_c:
        copy.wait_recv()
    for ox in range(3):
        near_y = [jnp.where(low, mrecv[side, ox, 1], mrecv[side, ox, 2]) for side in range(2)]
        far_y = [mrecv[side, ox, 0] for side in range(2)]
        for f in range(4):
            for x in range(4):
                s = 4 * f + x
                wd[f, 4 * ox + x, 0:8, 128:256] = rim(near_y[0], near_y[1], s)
                wd[f, 4 * ox + x, 8:16, 128:256] = rim(far_y[0], far_y[1], s)
    row16 = iota((16, 256), 0)
    lane16 = iota((16, 256), 1)
    y_at = gy * 4 + jnp.where(row16 < 8, row16, row16 - 16)
    z_at = gz * 128 + jnp.where(lane16 < 192, lane16, lane16 - 256)
    inside = (y_at >= 0) & (y_at < 4 * ng[1]) & (z_at >= 0) & (z_at < 128 * ng[2])
    inside = inside & ((row16 < 8) | (row16 >= 12)) & ((lane16 < 136) | (lane16 >= 248))
    inside = jnp.where(inside, 1, 0)

    @pl.loop(0, 12)
    def _(x):
        x_at = gx * 4 + x - 4
        x_in = jnp.where((x_at >= 0) & (x_at < 4 * ng[0]), 1, 0)
        wd[3, x] = jnp.where(inside * x_in > 0, wd[3, x], 0.0)

    @pl.loop(1, 11)
    def _(x):
        own, inverse = centre_terms(wd[3, x - 1], wd[3, x], wd[3, x + 1])
        cenw[x] = own
        dinvw[x] = inverse
        for c in range(3):
            m_b[c, x] = inverse * wd[c, x]

    for copy in loads[2:]:
        copy.wait()
    for copy in round_b:
        copy.wait_recv()
    g = own_g
    for k in range(len(column)):
        g = g + grecv[k]
    g = jnp.broadcast_to(g, (8, g.shape[1]))
    w = lax.dot_general(
        g, rows[...], (((1,), (1,)), ((), ())), precision=HIGH, preferred_element_type=F32
    )
    col = iota((16, 128), 1)
    blk = col // 24
    keep = (col < 72) & ((col % 24) // 2 == iota((16, 128), 0))
    keep = keep & ((blk != 0) | (gz > 0)) & ((blk != 2) | (gz < ng[2] - 1))
    picked = jnp.where(keep, jnp.broadcast_to(w[0:1, :], (16, 128)), 0.0)
    col = iota((128, 256), 0)
    quarter = iota((128, 256), 1) // 64
    code = 2 * (col // 24) + (col % 2)
    sel = jnp.where(code == jnp.where(quarter == 3, 1, quarter + 2), 1.0, 0.0)
    vown[...] = dot(picked, sel)
    round_d = [send(vown, vrecv.at[1 - d[0], 1 - d[1]], d) for d in flat]
    for copy in round_d:
        copy.wait_recv()

    row_in_8 = iota((8, 256), 0)
    for ox in range(3):
        x_at = gx + (ox - 1)
        x_in = (x_at >= 0) & (x_at < ng[0])
        values = []
        for oy in range(3):
            y_at = gy + (oy - 1)
            factor = jnp.where(x_in & (y_at >= 0) & (y_at < ng[1]), 1.0, 0.0)
            source = vown[...] if (ox, oy) == (1, 1) else vrecv[ox, oy]
            values.append(source * factor)
        for xb in range(2):
            for c in range(3):
                r = 4 * c + 2 * xb

                def line(oy, k, r=r, values=values):
                    return jnp.broadcast_to(values[oy][r + k : r + k + 1, :], (8, 256))

                upper_tile = jnp.where(
                    row_in_8 < 4,
                    jnp.where(row_in_8 < 2, line(1, 0), line(1, 1)),
                    jnp.where(row_in_8 < 6, line(2, 0), line(2, 1)),
                )
                lower_tile = jnp.where(row_in_8 < 6, line(0, 0), line(0, 1))
                for x in (4 * ox + 2 * xb, 4 * ox + 2 * xb + 1):
                    if 1 <= x < 11:
                        m_b[c, x, 0:8] += upper_tile
                        m_b[c, x, 8:16] += lower_tile

    @pl.loop(2, 10)
    def _(x):
        image = operate(lambda c, k: m_b[c, k], lambda k: wd[3, k], lambda k: cenw[k], x)
        for c in range(3):
            value = m_b[c, x] + dinvw[x] * (wd[c, x] - image[c])
            u8[c, x - 2] = jnp.where(row_in_8 < 6, value[0:8], value[8:16])

    fine_u = lax.dot_general(
        u8[...].reshape(192, 256), rz_mat[...], (((1,), (1,)), ((), ())),
        precision=HIGH, preferred_element_type=F32,
    ).reshape(3, 8, 8, 384)
    for t in range(3):
        piece = fine_u[:, :, :, 128 * t : 128 * t + 128]
        ysum[0:3, :, t, pl.ds(0, 8, stride=2), :] = piece
        ysum[0:3, :, t, pl.ds(1, 8, stride=2), :] = piece

    @pl.loop(1, 15)
    def _(x):
        k = x // 2
        for c in range(3):
            for t in range(3):
                lanes = slice(128 * t, 128 * t + 128)
                s_a[c, x, :, lanes] = s_b[c, x, :, lanes] + ysum[c, k, t]

    sweep(s_a, s_b, 2, 14)
    sweep(s_b, s_a, 3, 13)

    def last(x, sums):
        image = fine(s_a)(x + 4)
        new = list(sums)
        for c in range(3):
            p = s_a[c, x + 4, 0:8, 0:256]
            ap = image[c][0:8, 0:256]
            d = pdir[c, x]
            q = pimg[c, x]
            p_out[c, x] = p
            ap_out[c, x] = ap
            terms = (res[c, x + 4, 0:8, 0:256] * p, p * ap, p * q + d * ap, d * q)
            new = [a + b for a, b in zip(new, terms)]
        return tuple(new)

    zero = jnp.zeros((8, 256), F32)
    sums = lax.fori_loop(0, 8, last, (zero, zero, zero, zero))
    mine = jnp.zeros((8, 128), F32)
    for i, value in enumerate(sums):
        value = jnp.sum(value[:, 0:128] + value[:, 128:256], axis=0, keepdims=True)
        mine = jnp.where(row8 == i, jnp.broadcast_to(value, (8, 128)), mine)

    dsend[...] = mine
    copies = [send(dsend, drecv.at[k], d) for k, d in enumerate(layer)]
    for copy in copies:
        copy.wait_recv()
    for k in range(len(layer)):
        mine = mine + drecv[k]
    esend[...] = mine
    copies = [send(esend, erecv.at[k], d) for k, d in enumerate(column)]
    for copy in copies:
        copy.wait_recv()
    for k in range(len(column)):
        mine = mine + erecv[k]
    whole = jnp.broadcast_to(jnp.sum(mine, axis=1, keepdims=True), (8, 128))
    inner_rz, pp, cross, qq = (jnp.broadcast_to(whole[i : i + 1], (8, 128)) for i in range(4))
    beta = inner_rz / prev_rz[0]
    alpha = inner_rz / (pp + beta * (cross + beta * qq))
    ab_out[...] = jnp.where(row8 == 0, alpha, beta)
    for copy in started:
        copy.wait_send()


def solution(mesh):
    ng = tuple(mesh.shape[a] for a in AXES)

    def on_device(sol, res, pdir, pimg, prev_rz, dens, table, inverse):
        f = functools.partial(pltpu.VMEM, dtype=F32)

        def vm(*shape):
            return pltpu.VMEM(shape, F32)

        kc = inverse.shape[3]
        n_layer, n_col = ng[0] * ng[1] - 1, ng[2] - 1
        copies = 16 + 18 + 26 + 8 + n_layer + 2 * n_col
        scratch = [
            pltpu.VMEM((8, 8, 256), jnp.int32),
            vm(3, 16, 16, 384),
            vm(18, 24, 384),
            vm(18, 24, 384),
            vm(16, 16, 384), vm(16, 16, 384), vm(16, 16, 384),
            vm(3, 16, 16, 384), vm(3, 16, 16, 384),
            vm(3, 8, 8, 256), vm(3, 8, 8, 256),
            vm(2, 2, 8, 128), vm(2, 3, 3, 2, 8, 128),
            vm(4, 8, 3, 16, 128),
            vm(4, 8, 8, 256), vm(8, 8, 256), vm(8, 8, 256), vm(3, 8, 8, 256),
            vm(6, 8, 128),
            vm(2, 8, 128), vm(2, 3, 3, 8, 128),
            vm(4, 12, 16, 256), vm(12, 16, 256), vm(12, 16, 256),
            vm(3, 12, 16, 256), vm(8, 128), vm(3, 8, 8, 256),
            vm(384, 256),
            vm(1, kc), vm(n_col, 1, kc), vm(128, kc),
            vm(16, 256), vm(3, 3, 16, 256),
            vm(8, 128), vm(n_layer, 8, 128), vm(8, 128), vm(n_col, 8, 128),
            pltpu.SemaphoreType.DMA((7,)),
            pltpu.SemaphoreType.DMA((copies,)),
            pltpu.SemaphoreType.DMA((copies,)),
        ]
        anywhere = pl.BlockSpec(memory_space=pl.ANY)
        in_smem = pl.BlockSpec(memory_space=pltpu.SMEM)
        in_vmem = pl.BlockSpec(memory_space=pltpu.VMEM)
        field = jax.ShapeDtypeStruct(res.shape, F32)
        p, ap, ab = pl.pallas_call(
            functools.partial(kernel, ng),
            name="cg_step",
            out_shape=(field, field, jax.ShapeDtypeStruct((8, 128), F32)),
            in_specs=[anywhere] * 5 + [in_smem] * 2,
            out_specs=(in_vmem, in_vmem, in_vmem),
            scratch_shapes=scratch,
            compiler_params=pltpu.CompilerParams(
                collective_id=0, has_side_effects=True, vmem_limit_bytes=40 << 20
            ),
        )(res, pdir, pimg, dens, inverse, table, prev_rz.reshape(1))
        alpha, beta = ab[0, 0], ab[1, 0]
        direction = p + beta * pdir
        image = ap + beta * pimg
        return sol + alpha * direction, res - alpha * image, direction, image

    split = P(None, *AXES)
    return jax.shard_map(
        on_device,
        mesh=mesh,
        in_specs=(split, split, split, split, P(), P(*AXES), P(), P("gx", "gy", None, None)),
        out_specs=(split, split, split, split),
        check_vma=False,
    )
```

time: 475 us -> 76.3 us (0.16)
  blocking collectives: 188 us -> 0 us
  starting transfers between devices: 158 us -> 0 us
  Pallas kernels: 0 us -> 66.6 us
  waiting for transfers between devices: 47.4 us -> 0 us
  local copies, waits for them, and re-layouts: 39.9 us -> 5.9 us
  other arithmetic: 32.2 us -> 2.18 us
    psum x2 -> x0, blocking collectives: 164 us -> none  [the longest x1 87.9 us: on_device(): inner_rz = lax.psum(jnp.sum(residual * precond), ('gx', 'gy', 'gz'))]
    ppermute x54 -> x0, starting transfers between devices: 158 us -> none  [the longest x27 112 us: extended(): before = lax.ppermute(last, axis, up)]
    pallas_call x0 -> x1, Pallas kernels: none -> 66.6 us  [on_device(): pl.pallas_call(functools.partial(kernel, ng), name='cg_step', out_shape=(...]
    ppermute x54 -> x0, waiting for transfers between devices: 47.4 us -> none  [the longest x27 29.6 us: extended(): after = lax.ppermute(leading, axis, down)]
    reshape x4 -> x0, local copies, waits for them, and re-layouts: 29.5 us -> none  [the longest x1 14 us: boxed_sum(): field.reshape(3, field.shape[1] // box_x, box_x, field.shape[2] // box_y,...]
    unnamed x1 -> x0, blocking collectives: 24.4 us -> none
    mul x6 -> x0, other arithmetic: 11.2 us -> none  [the longest x1 11 us: diagonal_of(): total = MASS_SHIFT * coeff_centre]
    reduce_sum x5 -> x0, other arithmetic: 9.53 us -> none  [the longest x2 5.64 us: boxed_sum(): return jnp.sum(shaped, axis=(2, 4, 6))]
  transfers between devices with their start and end apart: 54 -> 0, of which waited for: 27 -> 0; matrix products, arithmetic and copies ran while one was open for 3% -> 0% of each run, Pallas kernels for 0% -> 0%
where the time goes in v1:
time: 76.3 us; the launch traced here: 76 us
  Pallas kernels  66.6 us (87%)
  local copies, waits for them, and re-layouts  5.9 us (8%)
  other arithmetic  2.18 us (3%)
  between operations  1.3 us (2%)
    pallas_call x1, Pallas kernels, on_device(): pl.pallas_call(functools.partial(kernel, ng), name='cg_step', out_shape=(...  66.6 us
    unnamed x14, local copies, waits for them, and re-layouts  5.33 us
    sub x1, other arithmetic, on_device(): return (sol + alpha * direction, res - alpha * image, direction, image)  2.18 us

profile of v1, /device:TPU:1, one launch (start us, length us, event | category | flops | bytes accessed | tf_op | source)
XLA Modules:
  0.0 76.0 jit_solution(1726627983496516438)
XLA Ops:
  1.3 0.0 copy-start.5
  1.3 0.6 copy-done.5
  1.9 0.0 copy-start
  1.9 0.9 %copy-done = f32[3,8,8,256]{3,2,1,0:T(8,128)S(1)} copy-done((f32[3,8,8,256]{3,2,1,0:T(8,128)S(1)}, f32[3,8,8,256]{3,2,1,0:T(8,128)}, u32[]{:S(2)}) %copy-start) | copy-done | bytes 196632
  2.9 0.0 copy-start.1
  2.9 0.9 %copy-done.1 = f32[3,8,8,256]{3,2,1,0:T(8,128)S(1)} copy-done((f32[3,8,8,256]{3,2,1,0:T(8,128)S(1)}, f32[3,8,8,256]{3,2,1,0:T(8,128)}, u32[]{:S(2)}) %copy-start.1) | copy-done | bytes 196632
  3.8 0.0 copy-start.2
  3.8 0.9 %copy-done.2 = f32[3,8,8,256]{3,2,1,0:T(8,128)S(1)} copy-done((f32[3,8,8,256]{3,2,1,0:T(8,128)S(1)}, f32[3,8,8,256]{3,2,1,0:T(8,128)}, u32[]{:S(2)}) %copy-start.2) | copy-done | bytes 196632
  4.7 0.0 copy-start.3
  4.7 1.1 %copy-done.3 = f32[1,1,384,384]{3,2,1,0:T(8,128)S(1)} copy-done((f32[1,1,384,384]{3,2,1,0:T(8,128)S(1)}, f32[1,1,384,384]{3,2,1,0:T(8,128)}, u32[]{:S(2)}) %copy-start.3) | copy-done | bytes 589848
  5.8 0.0 copy-start.4
  5.8 0.8 %copy-done.4 = s32[8,8,256]{2,1,0:T(8,128)S(1)} copy-done((s32[8,8,256]{2,1,0:T(8,128)S(1)}, s32[8,8,256]{2,1,0:T(8,128)}, u32[]{:S(2)}) %copy-start.4) | copy-done | bytes 65560
  6.6 0.0 copy-start.6
  6.6 66.6 %cg_step.1 = (f32[3,8,8,256]{3,2,1,0:T(8,128)S(1)}, f32[3,8,8,256]{3,2,1,0:T(8,128)S(1)}, f32[8,128]{1,0:T(8,128)S(1)}) custom-call(f32[3,8,8,256]{3,2,1,0:T(8,128)S(1)} %copy-done, f32[3,8,8,256]{3,2,1,0:T(8,128)S(1)} %copy-done.1, f32[3,8,8,256]{3,2,1,0:T(8,128)S(1)} %copy-done.2, s32[8,8,256]{2,1,0:T(8,128)S(1)} %copy-done.4, ...), custom_call_target="tpu_custom_call" | custom-call | tf_op jit(solution)/shard_map/cg_step/pallas_call | solution.py:529
  73.3 0.6 fusion
  73.8 0.0 copy-done.6
  73.8 2.2 %multiply_subtract_fusion = (f32[3,8,8,256]{3,2,1,0:T(8,128)}, f32[3,8,8,256]{3,2,1,0:T(8,128)}, f32[3,8,8,256]{3,2,1,0:T(8,128)}, f32[3,8,8,256]{3,2,1,0:T(8,128)}) fusion(f32[3,8,8,256]{3,2,1,0:T(8,128)S(1)} %copy-done, f32[]{:T(128)} %bitcast.1, f32[3,8,8,256]{3,2,1,0:T(8,128)S(1)} %get-tuple-element.9, f32[3,8,8,256]{3,2,1,0:T(8,128)S(1)} %copy-done.2, ...), kind=kLoop, calls=%fused_computation | loop fusion | flops 393216 | bytes 1966088 | tf_op jit(solution)/shard_map/sub | solution.py:543
Async XLA Ops:
  1.3 0.7 copy-start.5
  1.9 0.9 %copy-start = (f32[3,8,8,256]{3,2,1,0:T(8,128)S(1)}, f32[3,8,8,256]{3,2,1,0:T(8,128)}, u32[]{:S(2)}) copy-start(f32[3,8,8,256]{3,2,1,0:T(8,128)} %res_hbm.1) | copy-start | bytes 589828
  2.9 0.9 %copy-start.1 = (f32[3,8,8,256]{3,2,1,0:T(8,128)S(1)}, f32[3,8,8,256]{3,2,1,0:T(8,128)}, u32[]{:S(2)}) copy-start(f32[3,8,8,256]{3,2,1,0:T(8,128)} %dir_hbm.1) | copy-start | bytes 589828
  3.8 0.9 %copy-start.2 = (f32[3,8,8,256]{3,2,1,0:T(8,128)S(1)}, f32[3,8,8,256]{3,2,1,0:T(8,128)}, u32[]{:S(2)}) copy-start(f32[3,8,8,256]{3,2,1,0:T(8,128)} %img_hbm.1) | copy-start | bytes 589828
  4.7 1.1 %copy-start.3 = (f32[1,1,384,384]{3,2,1,0:T(8,128)S(1)}, f32[1,1,384,384]{3,2,1,0:T(8,128)}, u32[]{:S(2)}) copy-start(f32[1,1,384,384]{3,2,1,0:T(8,128)} %inv_hbm.1) | copy-start | bytes 1769476
  5.8 0.8 %copy-start.4 = (s32[8,8,256]{2,1,0:T(8,128)S(1)}, s32[8,8,256]{2,1,0:T(8,128)}, u32[]{:S(2)}) copy-start(s32[8,8,256]{2,1,0:T(8,128)} %dens_hbm.1) | copy-start | bytes 196612
  6.6 67.2 %copy-start.6 = (f32[3,8,8,256]{3,2,1,0:T(8,128)S(1)}, f32[3,8,8,256]{3,2,1,0:T(8,128)}, u32[]{:S(2)}) copy-start(f32[3,8,8,256]{3,2,1,0:T(8,128)} %param.8) | copy-start | bytes 589828

commit v2 on v1

--- a/solution.py
+++ b/solution.py
@@ -15,6 +15,7 @@
 F32 = jnp.float32
 HIGH = lax.Precision.HIGHEST
 DAMP = 0.6
+UNROLL = 2
 EIGHTIETH = 0.0125
 SMALL = (-1, 0, 1)
 
@@ -58,13 +59,13 @@
 
 def kernel(
     ng,
-    res_hbm, dir_hbm, img_hbm, dens_hbm, inv_hbm, table, prev_rz,
-    p_out, ap_out, ab_out,
-    dens, res, ewide, emask, e16, cen, dinv, s_a, s_b, pdir, pimg,
+    res_hbm, dir_hbm, img_hbm, dens_hbm, inv_hbm, table_hbm, rz_hbm,
+    p_hbm, ap_hbm, ab_out,
+    dens, res, ewide, e16, cen, dinv, s_a, s_b, pdir, pimg,
     spack, srecv, ysum, km, cen1, dinv1, m_a, tlow,
     mpack, mrecv, wd, cenw, dinvw, m_b, m_c, u8,
-    rz_mat, gsend, grecv, rows, vown, vrecv,
-    dsend, drecv, esend, erecv,
+    rz_mat, sel, gsend, grecv, rows, wsend, wrecv,
+    dsend, drecv, esend, erecv, p_out, ap_out, table, prev_rz,
     lsem, sems, recs,
 ):
     gx, gy, gz = (lax.axis_index(a) for a in AXES)
@@ -73,25 +74,31 @@
     def device(d):
         return tuple(lax.rem(me[i] + (d[i] % ng[i]), ng[i]) for i in range(3))
 
+    def hops(d):
+        return sum(min(d[i] % ng[i], -d[i] % ng[i]) for i in range(3))
+
     near = [d for d in itertools.product(SMALL, repeat=3) if d != (0, 0, 0)]
+    near.sort(key=hops, reverse=True)
     flat = [d for d in near if d[2] == 0]
-    column = [(0, 0, k) for k in range(1, ng[2])]
+    tilted = [d for d in near if d[2] != 0]
+    column = sorted(((0, 0, k) for k in range(1, ng[2])), key=hops, reverse=True)
     layer = [(i, j, 0) for i in range(ng[0]) for j in range(ng[1]) if (i, j) != (0, 0)]
+    layer.sort(key=hops, reverse=True)
     partners = []
     for d in near + column + layer:
         d = tuple(d[i] % ng[i] for i in range(3))
         if d not in partners:
             partners.append(d)
 
-    barrier = pltpu.get_barrier_semaphore()
-    for d in partners:
-        pl.semaphore_signal(barrier, inc=1, device_id=device(d), device_id_type=MESH)
     loads = [
         pltpu.make_async_copy(dens_hbm, dens, lsem.at[0]),
         pltpu.make_async_copy(res_hbm, res.at[:, 4:12, 0:8, 0:256], lsem.at[1]),
         pltpu.make_async_copy(dir_hbm, pdir, lsem.at[2]),
         pltpu.make_async_copy(img_hbm, pimg, lsem.at[3]),
+        pltpu.make_async_copy(rz_hbm, prev_rz, lsem.at[8]),
     ]
+    table_load = pltpu.make_async_copy(table_hbm, table, lsem.at[7])
+    table_load.start()
     for b in range(3):
         block = jnp.clip(gz + (b - 1), 0, ng[2] - 1)
         start = pl.multiple_of(block * 24, 8)
@@ -102,10 +109,14 @@
         )
     for copy in loads:
         copy.start()
+    barrier = pltpu.get_barrier_semaphore()
+    for d in partners:
+        pl.semaphore_signal(barrier, inc=1, device_id=device(d), device_id_type=MESH)
     rows[72:128, :] = jnp.zeros((56, rows.shape[1]), F32)
+    table_load.wait()
     loads[0].wait()
 
-    @pl.loop(0, 8)
+    @pl.loop(0, 8, unroll=4)
     def _(x):
         index = dens[x]
         young = jnp.full(index.shape, table[0], F32)
@@ -126,14 +137,13 @@
 
     for side, (at, extra) in enumerate(((0, 0), (128, 8))):
         for t in range(2):
-            def pack_one(x, total, t=t, at=at, extra=extra):
-                for k in range(2):
+            total = jnp.zeros((8, 128), F32)
+            for k in range(2):
+                for x in range(8):
                     s = k * 8 + x
-                    moved = pltpu.roll(fine_tile(2 * t + k, x, at), lax.rem(8 * s + extra, 128), 1)
+                    moved = pltpu.roll(fine_tile(2 * t + k, x, at), (8 * s + extra) % 128, 1)
                     total = jnp.where(slot8 == s, moved, total)
-                return total
-
-            spack[side, t] = lax.fori_loop(0, 8, pack_one, jnp.zeros((8, 128), F32))
+            spack[side, t] = total
 
     pl.semaphore_wait(barrier, len(partners))
 
@@ -151,7 +161,6 @@
         started.append(copy)
         return copy
 
-    round_a = []
     pick = {
         -1: (slice(4, 8), slice(12, 16)), 0: (slice(4, 12), slice(4, 12)), 1: (slice(8, 12), slice(0, 4)),
     }
@@ -159,45 +168,49 @@
     pick_e = {
         -1: (slice(5, 10), slice(13, 18)), 0: (slice(5, 13), slice(5, 13)), 1: (slice(8, 13), slice(0, 5)),
     }
-    pick_e_row = {-1: slice(16, 24), 0: slice(8, 16), 1: slice(0, 8)}
+    pick_e_row = {
+        -1: (slice(8, 13), slice(16, 21)), 0: (slice(8, 16), slice(8, 16)), 1: (slice(11, 16), slice(3, 8)),
+    }
     main = slice(0, 256)
+    round_z, round_e, round_r = [], [], []
+    for d in tilted:
+        side = 0 if d[2] < 0 else 1
+        round_z.append(send(spack.at[side], srecv.at[side, 1 - d[0], 1 - d[1]], d))
+    for d in flat:
+        src = ewide.at[pick_e[d[0]][0], pick_e_row[d[1]][0], main]
+        dst = ewide.at[pick_e[d[0]][1], pick_e_row[d[1]][1], main]
+        round_e.append(send(src, dst, d))
     for d in flat:
         src = res.at[:, pick[d[0]][0], pick_row[d[1]][0], main]
         dst = res.at[:, pick[d[0]][1], pick_row[d[1]][1], main]
-        round_a.append(send(src, dst, d))
-    for d in flat:
-        src = ewide.at[pick_e[d[0]][0], slice(8, 16), main]
-        dst = ewide.at[pick_e[d[0]][1], pick_e_row[d[1]], main]
-        round_a.append(send(src, dst, d))
-    for d in near:
-        if d[2] != 0:
-            side = 0 if d[2] < 0 else 1
-            round_a.append(send(spack.at[side], srecv.at[side, 1 - d[0], 1 - d[1]], d))
+        round_r.append(send(src, dst, d))
 
     lane_of = iota((384, 256), 0)
     target = jnp.where(lane_of < 320, lane_of // 2, lane_of // 2 + 64)
     rz_mat[...] = jnp.where(iota((384, 256), 1) == target, 1.0, 0.0)
 
-    for copy in round_a:
+    col = iota((128, 256), 0)
+    quarter = iota((128, 256), 1) // 64
+    code = 2 * (col // 24) + (col % 2)
+    sel[...] = jnp.where(code == jnp.where(quarter == 3, 1, quarter + 2), 1.0, 0.0)
+
+    for copy in round_z:
         copy.wait_recv()
 
     def rim(right, left, s):
-        to_right = pltpu.roll(right, lax.rem(256 - 8 * s, 128), 1)
-        to_left = pltpu.roll(left, lax.rem(256 - 8 * s - 8, 128), 1)
+        to_right = pltpu.roll(right, (-8 * s) % 128, 1)
+        to_left = pltpu.roll(left, (-8 * s - 8) % 128, 1)
         return jnp.where(lane8 < 64, to_right, to_left)
 
     rim_lanes = slice(256, 384)
     for ox, first, count, base in ((-1, 4, 4, 0), (0, 0, 8, 4), (1, 0, 4, 12)):
         for t in range(2):
-            tiles = []
-            for side in range(2):
-                tiles.append(srecv[side, ox + 1, 1, t] if True else None)
+            tiles = [srecv[side, ox + 1, 1, t] for side in range(2)]
             mixed = [
                 jnp.where(row8 < 4, srecv[side, ox + 1, 2, t], srecv[side, ox + 1, 0, t]) for side in range(2)
             ]
 
-            @pl.loop(0, count)
-            def _(i, t=t, first=first, base=base, tiles=tiles, mixed=mixed):
+            for i in range(count):
                 for k in range(2):
                     if 2 * t + k < 3:
                         s = k * 8 + first + i
@@ -207,8 +220,7 @@
     for ox, first, count, base in ((-1, 3, 5, 0), (0, 0, 8, 5), (1, 0, 5, 13)):
         tiles = [[srecv[side, ox + 1, oy, 1] for side in range(2)] for oy in range(3)]
 
-        @pl.loop(0, count)
-        def _(i, first=first, base=base, tiles=tiles):
+        for i in range(count):
             for oy in range(3):
                 ewide[base + i, 8 * oy : 8 * oy + 8, rim_lanes] = rim(tiles[oy][0], tiles[oy][1], 8 + first + i)
 
@@ -217,23 +229,37 @@
     y_at = gy * 8 + row24 - 8
     z_at = gz * 256 + jnp.where(lane24 < 320, lane24, lane24 - 384)
     inside = (y_at >= 0) & (y_at < 8 * ng[1]) & (z_at >= 0) & (z_at < 256 * ng[2])
-    inside = jnp.where(inside & ((lane24 < 264) | (lane24 >= 376)), 1, 0)
-
-    @pl.loop(0, 18)
-    def _(x):
+    inside = inside & ((lane24 < 264) | (lane24 >= 376)) & (row24 >= 3) & (row24 < 21)
+    inside = jnp.where(inside, 1, 0)
+    for copy in round_e:
+        copy.wait_recv()
+    upper = iota((8, 384), 0) < 4
+
+    def fold(value):
+        return jnp.concatenate([value[8:16], jnp.where(upper, value[16:24], value[0:8])], axis=0)
+
+    def masked(x):
         x_at = gx * 8 + x - 5
         x_in = jnp.where((x_at >= 0) & (x_at < 8 * ng[0]), 1, 0)
-        emask[x] = jnp.where(inside * x_in > 0, ewide[x], 0.0)
-
-    upper = iota((8, 384), 0) < 4
-
-    @pl.loop(0, 16)
+        return jnp.where(inside * x_in > 0, ewide[x], 0.0)
+
+    @pl.loop(0, 16, unroll=2)
     def _(x):
-        mid = emask[x + 1]
-        own, inverse = centre_terms(emask[x], mid, emask[x + 2])
-        for value, out in ((mid, e16), (own, cen), (inverse, dinv)):
-            out[x, 0:8, :] = value[8:16]
-            out[x, 8:16, :] = jnp.where(upper, value[16:24], value[0:8])
+        low, mid, high = masked(x), masked(x + 1), masked(x + 2)
+        wide = three(low, mid, high)
+        wide = fold((wide + wide) + (pltpu.roll(wide, 1, 0) + pltpu.roll(wide, 23, 0)))
+        wide = EIGHTIETH * ((wide + wide) + (pltpu.roll(wide, 1, 1) + pltpu.roll(wide, 383, 1)))
+        mid = fold(mid)
+        inverse = jnp.where(mid > 0.0, DAMP / (0.7 * mid + wide), 0.0)
+        e16[x] = mid
+        cen[x] = 0.9 * mid + wide
+        dinv[x] = inverse
+
+    for copy in round_r:
+        copy.wait_recv()
+
+    @pl.loop(0, 16, unroll=4)
+    def _(x):
         for c in range(3):
             s_a[c, x] = dinv[x] * res[c, x]
 
@@ -243,7 +269,7 @@
         )
 
     def sweep(source, out, start, stop):
-        @pl.loop(start, stop)
+        @pl.loop(start, stop, unroll=UNROLL)
         def _(x):
             image = fine(source)(x)
             for c in range(3):
@@ -263,7 +289,7 @@
             both = (res[c, x] - first[c]) + (res[c, x + 1] - second[c])
             put_tiles(ysum, c, k + 1, both + pltpu.roll(both, 15, 0))
 
-    @pl.loop(0, 8)
+    @pl.loop(0, 8, unroll=4)
     def _(k):
         both = e16[2 * k] + e16[2 * k + 1]
         put_tiles(ysum, 3, k, both + pltpu.roll(both, 15, 0))
@@ -281,7 +307,7 @@
     km[0:3] = 0.5 * total[0:3]
     km[3] = 0.125 * total[3]
 
-    @pl.loop(1, 7)
+    @pl.loop(1, 7, unroll=3)
     def _(k):
         own, inverse = centre_terms(km[3, k - 1], km[3, k], km[3, k + 1])
         cen1[k] = own
@@ -326,13 +352,26 @@
     block = km.at[:, 2:6, 0:4, 0:128]
     for d in flat:
         round_c.append(send(block, wd.at[:, mid_x[d[0]], mid_row[d[1]], 0:128], d))
-    for d in near:
-        if d[2] != 0:
-            side = 0 if d[2] < 0 else 1
-            round_c.append(send(mpack.at[side], mrecv.at[side, 1 - d[0], 1 - d[1]], d))
+    for d in tilted:
+        side = 0 if d[2] < 0 else 1
+        round_c.append(send(mpack.at[side], mrecv.at[side, 1 - d[0], 1 - d[1]], d))
     for f in range(4):
         wd[f, 4:8, 0:4, 0:128] = km[f, 2:6, 0:4, 0:128]
         wd[f, :, 8:12, 0:128] = jnp.zeros((12, 4, 128), F32)
+    for copy in loads[2:]:
+        copy.wait()
+    for copy in round_b:
+        copy.wait_recv()
+    g = own_g
+    for k in range(len(column)):
+        g = g + grecv[k]
+    g = jnp.broadcast_to(g, (8, g.shape[1]))
+    w = lax.dot_general(
+        g, rows[...], (((1,), (1,)), ((), ())), precision=HIGH, preferred_element_type=F32
+    )
+    wsend[...] = w[0:1, :]
+    round_d = [send(wsend, wrecv.at[1 - d[0], 1 - d[1]], d) for d in flat]
+
     for copy in round_c:
         copy.wait_recv()
     for ox in range(3):
@@ -351,13 +390,13 @@
     inside = inside & ((row16 < 8) | (row16 >= 12)) & ((lane16 < 136) | (lane16 >= 248))
     inside = jnp.where(inside, 1, 0)
 
-    @pl.loop(0, 12)
+    @pl.loop(0, 12, unroll=4)
     def _(x):
         x_at = gx * 4 + x - 4
         x_in = jnp.where((x_at >= 0) & (x_at < 4 * ng[0]), 1, 0)
         wd[3, x] = jnp.where(inside * x_in > 0, wd[3, x], 0.0)
 
-    @pl.loop(1, 11)
+    @pl.loop(1, 11, unroll=2)
     def _(x):
         own, inverse = centre_terms(wd[3, x - 1], wd[3, x], wd[3, x + 1])
         cenw[x] = own
@@ -365,41 +404,25 @@
         for c in range(3):
             m_b[c, x] = inverse * wd[c, x]
 
-    for copy in loads[2:]:
-        copy.wait()
-    for copy in round_b:
-        copy.wait_recv()
-    g = own_g
-    for k in range(len(column)):
-        g = g + grecv[k]
-    g = jnp.broadcast_to(g, (8, g.shape[1]))
-    w = lax.dot_general(
-        g, rows[...], (((1,), (1,)), ((), ())), precision=HIGH, preferred_element_type=F32
-    )
     col = iota((16, 128), 1)
     blk = col // 24
     keep = (col < 72) & ((col % 24) // 2 == iota((16, 128), 0))
     keep = keep & ((blk != 0) | (gz > 0)) & ((blk != 2) | (gz < ng[2] - 1))
-    picked = jnp.where(keep, jnp.broadcast_to(w[0:1, :], (16, 128)), 0.0)
-    col = iota((128, 256), 0)
-    quarter = iota((128, 256), 1) // 64
-    code = 2 * (col // 24) + (col % 2)
-    sel = jnp.where(code == jnp.where(quarter == 3, 1, quarter + 2), 1.0, 0.0)
-    vown[...] = dot(picked, sel)
-    round_d = [send(vown, vrecv.at[1 - d[0], 1 - d[1]], d) for d in flat]
     for copy in round_d:
         copy.wait_recv()
+    picked = []
+    for ox in range(3):
+        for oy in range(3):
+            x_at, y_at = gx + (ox - 1), gy + (oy - 1)
+            known = (x_at >= 0) & (x_at < ng[0]) & (y_at >= 0) & (y_at < ng[1])
+            line = wsend[...] if (ox, oy) == (1, 1) else wrecv[ox, oy]
+            line = jnp.broadcast_to(line * jnp.where(known, 1.0, 0.0), (16, 128))
+            picked.append(jnp.where(keep, line, 0.0))
+    blocks = dot(jnp.concatenate(picked, axis=0), sel[...])
 
     row_in_8 = iota((8, 256), 0)
     for ox in range(3):
-        x_at = gx + (ox - 1)
-        x_in = (x_at >= 0) & (x_at < ng[0])
-        values = []
-        for oy in range(3):
-            y_at = gy + (oy - 1)
-            factor = jnp.where(x_in & (y_at >= 0) & (y_at < ng[1]), 1.0, 0.0)
-            source = vown[...] if (ox, oy) == (1, 1) else vrecv[ox, oy]
-            values.append(source * factor)
+        values = [blocks[16 * (3 * ox + oy) : 16 * (3 * ox + oy) + 16] for oy in range(3)]
         for xb in range(2):
             for c in range(3):
                 r = 4 * c + 2 * xb
@@ -418,7 +441,7 @@
                         m_b[c, x, 0:8] += upper_tile
                         m_b[c, x, 8:16] += lower_tile
 
-    @pl.loop(2, 10)
+    @pl.loop(2, 10, unroll=UNROLL)
     def _(x):
         image = operate(lambda c, k: m_b[c, k], lambda k: wd[3, k], lambda k: cenw[k], x)
         for c in range(3):
@@ -434,7 +457,7 @@
         ysum[0:3, :, t, pl.ds(0, 8, stride=2), :] = piece
         ysum[0:3, :, t, pl.ds(1, 8, stride=2), :] = piece
 
-    @pl.loop(1, 15)
+    @pl.loop(1, 15, unroll=2)
     def _(x):
         k = x // 2
         for c in range(3):
@@ -460,39 +483,83 @@
         return tuple(new)
 
     zero = jnp.zeros((8, 256), F32)
-    sums = lax.fori_loop(0, 8, last, (zero, zero, zero, zero))
-    mine = jnp.zeros((8, 128), F32)
+    stores = [
+        pltpu.make_async_copy(p_out, p_hbm, lsem.at[0]),
+        pltpu.make_async_copy(ap_out, ap_hbm, lsem.at[1]),
+    ]
+    sums = lax.fori_loop(0, 8, last, (zero, zero, zero, zero), unroll=UNROLL)
+    group = iota((1, 128), 1) // 32
+    mine = jnp.zeros((1, 128), F32)
     for i, value in enumerate(sums):
         value = jnp.sum(value[:, 0:128] + value[:, 128:256], axis=0, keepdims=True)
-        mine = jnp.where(row8 == i, jnp.broadcast_to(value, (8, 128)), mine)
-
-    dsend[...] = mine
-    copies = [send(dsend, drecv.at[k], d) for k, d in enumerate(layer)]
-    for copy in copies:
-        copy.wait_recv()
-    for k in range(len(layer)):
-        mine = mine + drecv[k]
-    esend[...] = mine
-    copies = [send(esend, erecv.at[k], d) for k, d in enumerate(column)]
-    for copy in copies:
-        copy.wait_recv()
-    for k in range(len(column)):
-        mine = mine + erecv[k]
-    whole = jnp.broadcast_to(jnp.sum(mine, axis=1, keepdims=True), (8, 128))
-    inner_rz, pp, cross, qq = (jnp.broadcast_to(whole[i : i + 1], (8, 128)) for i in range(4))
+        value = value + pltpu.roll(value, 64, 1)
+        value = value + pltpu.roll(value, 32, 1)
+        mine = jnp.where(group == i, value, mine)
+
+    for peers, out, into in ((layer, dsend, drecv), (column, esend, erecv)):
+        out[...] = mine
+        copies = [send(out, into.at[k], d) for k, d in enumerate(peers)]
+        if peers is layer:
+            for copy in stores:
+                copy.start()
+        for copy in copies:
+            copy.wait_recv()
+        for k in range(len(peers)):
+            mine = mine + into[k]
+    inner_rz, pp, cross, qq = (
+        jnp.sum(jnp.where(group == i, mine, 0.0), axis=1, keepdims=True) for i in range(4)
+    )
     beta = inner_rz / prev_rz[0]
     alpha = inner_rz / (pp + beta * (cross + beta * qq))
-    ab_out[...] = jnp.where(row8 == 0, alpha, beta)
+    ab_out[...] = jnp.where(group < 2, alpha, beta)
+    for copy in stores:
+        copy.wait()
     for copy in started:
         copy.wait_send()
 
 
+def finish(
+    *refs,
+):
+    sources, ab_hbm, targets = refs[0:6], refs[6], refs[7:11]
+    held, ab, made, sems, outs = refs[11:17], refs[17], refs[18:22], refs[22], refs[23]
+    ab_load = pltpu.make_async_copy(ab_hbm, ab, sems.at[3, 0])
+    ab_load.start()
+    loads = [
+        [pltpu.make_async_copy(src.at[c], dst.at[c], sems.at[c, i]) for i, (src, dst) in enumerate(zip(sources, held))]
+        for c in range(3)
+    ]
+    for part in loads:
+        for copy in part:
+            copy.start()
+    pdir, pimg, sol, res, p, ap = held
+    new_sol, new_res, new_dir, new_img = made
+    ab_load.wait()
+    alpha = jnp.broadcast_to(ab[0:1, 0:1], (8, 256))
+    beta = jnp.broadcast_to(ab[0:1, 64:65], (8, 256))
+    stores = []
+    for c in range(3):
+        for copy in loads[c]:
+            copy.wait()
+        for x in range(p.shape[1]):
+            direction = p[c, x] + beta * pdir[c, x]
+            image = ap[c, x] + beta * pimg[c, x]
+            new_dir[c, x] = direction
+            new_img[c, x] = image
+            new_sol[c, x] = sol[c, x] + alpha * direction
+            new_res[c, x] = res[c, x] - alpha * image
+        for i, (src, dst) in enumerate(zip(made, targets)):
+            copy = pltpu.make_async_copy(src.at[c], dst.at[c], outs.at[c, i])
+            copy.start()
+            stores.append(copy)
+    for copy in stores:
+        copy.wait()
+
+
 def solution(mesh):
     ng = tuple(mesh.shape[a] for a in AXES)
 
     def on_device(sol, res, pdir, pimg, prev_rz, dens, table, inverse):
-        f = functools.partial(pltpu.VMEM, dtype=F32)
-
         def vm(*shape):
             return pltpu.VMEM(shape, F32)
 
@@ -502,7 +569,6 @@
         scratch = [
             pltpu.VMEM((8, 8, 256), jnp.int32),
             vm(3, 16, 16, 384),
-            vm(18, 24, 384),
             vm(18, 24, 384),
             vm(16, 16, 384), vm(16, 16, 384), vm(16, 16, 384),
             vm(3, 16, 16, 384), vm(3, 16, 16, 384),
@@ -514,33 +580,40 @@
             vm(2, 8, 128), vm(2, 3, 3, 8, 128),
             vm(4, 12, 16, 256), vm(12, 16, 256), vm(12, 16, 256),
             vm(3, 12, 16, 256), vm(8, 128), vm(3, 8, 8, 256),
-            vm(384, 256),
+            vm(384, 256), vm(128, 256),
             vm(1, kc), vm(n_col, 1, kc), vm(128, kc),
-            vm(16, 256), vm(3, 3, 16, 256),
-            vm(8, 128), vm(n_layer, 8, 128), vm(8, 128), vm(n_col, 8, 128),
-            pltpu.SemaphoreType.DMA((7,)),
+            vm(1, 128), vm(3, 3, 1, 128),
+            vm(1, 128), vm(n_layer, 1, 128), vm(1, 128), vm(n_col, 1, 128),
+            vm(3, 8, 8, 256), vm(3, 8, 8, 256),
+            pltpu.SMEM(table.shape, F32), pltpu.SMEM((1,), F32),
+            pltpu.SemaphoreType.DMA((9,)),
             pltpu.SemaphoreType.DMA((copies,)),
             pltpu.SemaphoreType.DMA((copies,)),
         ]
-        anywhere = pl.BlockSpec(memory_space=pl.ANY)
-        in_smem = pl.BlockSpec(memory_space=pltpu.SMEM)
+        in_hbm = pl.BlockSpec(memory_space=pltpu.HBM)
         in_vmem = pl.BlockSpec(memory_space=pltpu.VMEM)
         field = jax.ShapeDtypeStruct(res.shape, F32)
         p, ap, ab = pl.pallas_call(
             functools.partial(kernel, ng),
             name="cg_step",
-            out_shape=(field, field, jax.ShapeDtypeStruct((8, 128), F32)),
-            in_specs=[anywhere] * 5 + [in_smem] * 2,
-            out_specs=(in_vmem, in_vmem, in_vmem),
+            out_shape=(field, field, jax.ShapeDtypeStruct((1, 128), F32)),
+            in_specs=[in_hbm] * 7,
+            out_specs=(in_hbm, in_hbm, in_vmem),
             scratch_shapes=scratch,
             compiler_params=pltpu.CompilerParams(
-                collective_id=0, has_side_effects=True, vmem_limit_bytes=40 << 20
+                collective_id=0, has_side_effects=True, vmem_limit_bytes=56 << 20
             ),
         )(res, pdir, pimg, dens, inverse, table, prev_rz.reshape(1))
-        alpha, beta = ab[0, 0], ab[1, 0]
-        direction = p + beta * pdir
-        image = ap + beta * pimg
-        return sol + alpha * direction, res - alpha * image, direction, image
+        return pl.pallas_call(
+            finish,
+            name="cg_finish",
+            out_shape=(field,) * 4,
+            in_specs=[in_hbm] * 7,
+            out_specs=(in_hbm,) * 4,
+            scratch_shapes=[vm(*res.shape)] * 6 + [vm(1, 128)] + [vm(*res.shape)] * 4
+            + [pltpu.SemaphoreType.DMA((4, 6)), pltpu.SemaphoreType.DMA((3, 4))],
+            compiler_params=pltpu.CompilerParams(vmem_limit_bytes=56 << 20),
+        )(pdir, pimg, sol, res, p, ap, ab)
 
     split = P(None, *AXES)
     return jax.shard_map(

time: 76.3 us -> 56.7 us (0.74)
  Pallas kernels: 66.6 us -> 55.2 us
  local copies, waits for them, and re-layouts: 5.9 us -> 0 us
  other arithmetic: 2.18 us -> 0 us
    pallas_call x1, Pallas kernels: 66.6 us -> 52.9 us  [on_device(): pl.pallas_call(functools.partial(kernel, ng), name='cg_step', out_shape=(...]
    unnamed x14 -> x0, local copies, waits for them, and re-layouts: 5.33 us -> none
    pallas_call x0 -> x1, Pallas kernels: none -> 2.31 us  [on_device(): pl.pallas_call(finish, name='cg_finish', out_shape=(field,) * 4, in_specs...]
    sub x1 -> x0, other arithmetic: 2.18 us -> none  [on_device(): return (sol + alpha * direction, res - alpha * image, direction, image)]
where the time goes in v2:
time: 56.7 us; the launch traced here: 56.5 us
  Pallas kernels  55.2 us (97%)
  between operations  1.28 us (2%)
    pallas_call x1, Pallas kernels, on_device(): pl.pallas_call(functools.partial(kernel, ng), name='cg_step', out_shape=(...  52.9 us
    pallas_call x1, Pallas kernels, on_device(): pl.pallas_call(finish, name='cg_finish', out_shape=(field,) * 4, in_specs...  2.31 us

profile of v2, /device:TPU:1, one launch (start us, length us, event | category | flops | bytes accessed | tf_op | source)
XLA Modules:
  0.0 56.5 jit_solution(17557794165939314376)
XLA Ops:
  1.3 52.9 %cg_step.1 = (f32[3,8,8,256]{3,2,1,0:T(8,128)}, f32[3,8,8,256]{3,2,1,0:T(8,128)}, f32[1,128]{1,0:T(1,128)}) custom-call(f32[3,8,8,256]{3,2,1,0:T(8,128)} %refs_3_.1, f32[3,8,8,256]{3,2,1,0:T(8,128)} %refs_0_.1, f32[3,8,8,256]{3,2,1,0:T(8,128)} %refs_1_.1, s32[8,8,256]{2,1,0:T(8,128)} %dens_hbm.1, f32[1,1,384,384]{3,2,1,0:T(8,128)} %inv_hbm.1, f32[16]{0:T(128)} %table_hbm.1, ...), custom_call_target="tpu_custom_call" | custom-call | tf_op jit(solution)/shard_map/cg_step/pallas_call | solution.py:596
  54.2 2.3 %cg_finish.1 = (f32[3,8,8,256]{3,2,1,0:T(8,128)}, f32[3,8,8,256]{3,2,1,0:T(8,128)}, f32[3,8,8,256]{3,2,1,0:T(8,128)}, f32[3,8,8,256]{3,2,1,0:T(8,128)}) custom-call(f32[3,8,8,256]{3,2,1,0:T(8,128)} %refs_0_.1, f32[3,8,8,256]{3,2,1,0:T(8,128)} %refs_1_.1, f32[3,8,8,256]{3,2,1,0:T(8,128)} %refs_2_.1, f32[3,8,8,256]{3,2,1,0:T(8,128)} %refs_3_.1, ...), custom_call_target="tpu_custom_call" | custom-call | tf_op jit(solution)/shard_map/cg_finish/pallas_call | solution.py:607

commit v3 on v2

--- a/solution.py
+++ b/solution.py
@@ -16,6 +16,7 @@
 HIGH = lax.Precision.HIGHEST
 DAMP = 0.6
 UNROLL = 2
+STEP = 2
 EIGHTIETH = 0.0125
 SMALL = (-1, 0, 1)
 
@@ -34,17 +35,24 @@
     return (mid + mid) + (low + high)
 
 
-def operate(field, coeff, centre, at):
-    e_low, e_mid, e_high = coeff(at - 1), coeff(at), coeff(at + 1)
-    own = centre(at)
-    parts = []
+def operate(field, coeff, centre, at, count):
+    planes = range(count + 2)
+    e = [coeff(at - 1 + i) for i in planes]
+    parts = [[] for _ in range(count)]
     for c in range(3):
-        low, mid, high = field(c, at - 1), field(c, at), field(c, at + 1)
-        plain = smooth_rows_lanes(three(low, mid, high))
-        scaled = smooth_rows_lanes(three(e_low * low, e_mid * mid, e_high * high))
-        parts.append(own * mid - EIGHTIETH * (e_mid * plain + scaled))
-    shared = 0.3 * (parts[0] + parts[1] + parts[2])
-    return [0.7 * part + shared for part in parts]
+        v = [field(c, at - 1 + i) for i in planes]
+        ev = [e[i] * v[i] for i in planes]
+        pair = [v[i] + v[i + 1] for i in range(count + 1)]
+        epair = [ev[i] + ev[i + 1] for i in range(count + 1)]
+        for i in range(count):
+            plain = smooth_rows_lanes(pair[i] + pair[i + 1])
+            scaled = smooth_rows_lanes(epair[i] + epair[i + 1])
+            parts[i].append(centre(at + i) * v[i + 1] - EIGHTIETH * (e[i + 1] * plain + scaled))
+    images = []
+    for part in parts:
+        shared = 0.3 * (part[0] + part[1] + part[2])
+        images.append([0.7 * piece + shared for piece in part])
+    return images
 
 
 def centre_terms(low, mid, high):
@@ -53,8 +61,15 @@
     return 0.9 * mid + wide, inverse
 
 
-def dot(a, b):
-    return jnp.dot(a, b, precision=HIGH, preferred_element_type=F32)
+def dot(a, b, dims=(((1,), (0,)), ((), ()))):
+    total = None
+    for part in range(3):
+        piece = a.astype(jnp.bfloat16)
+        term = lax.dot_general(piece, b, dims, preferred_element_type=F32)
+        total = term if total is None else total + term
+        if part < 2:
+            a = a - piece.astype(F32)
+    return total
 
 
 def kernel(
@@ -64,7 +79,7 @@
     dens, res, ewide, e16, cen, dinv, s_a, s_b, pdir, pimg,
     spack, srecv, ysum, km, cen1, dinv1, m_a, tlow,
     mpack, mrecv, wd, cenw, dinvw, m_b, m_c, u8,
-    rz_mat, sel, gsend, grecv, rows, wsend, wrecv,
+    rz_mat, sel, halves, keep48, gsend, grecv, rows, wsend, wrecv,
     dsend, drecv, esend, erecv, p_out, ap_out, table, prev_rz,
     lsem, sems, recs,
 ):
@@ -172,7 +187,7 @@
         -1: (slice(8, 13), slice(16, 21)), 0: (slice(8, 16), slice(8, 16)), 1: (slice(11, 16), slice(3, 8)),
     }
     main = slice(0, 256)
-    round_z, round_e, round_r = [], [], []
+    round_z, round_e, round_y, round_r = [], [], [], []
     for d in tilted:
         side = 0 if d[2] < 0 else 1
         round_z.append(send(spack.at[side], srecv.at[side, 1 - d[0], 1 - d[1]], d))
@@ -180,19 +195,26 @@
         src = ewide.at[pick_e[d[0]][0], pick_e_row[d[1]][0], main]
         dst = ewide.at[pick_e[d[0]][1], pick_e_row[d[1]][1], main]
         round_e.append(send(src, dst, d))
-    for d in flat:
+    for d in reversed(flat):
         src = res.at[:, pick[d[0]][0], pick_row[d[1]][0], main]
         dst = res.at[:, pick[d[0]][1], pick_row[d[1]][1], main]
-        round_r.append(send(src, dst, d))
+        (round_y if d[0] == 0 else round_r).append(send(src, dst, d))
 
     lane_of = iota((384, 256), 0)
     target = jnp.where(lane_of < 320, lane_of // 2, lane_of // 2 + 64)
-    rz_mat[...] = jnp.where(iota((384, 256), 1) == target, 1.0, 0.0)
+    rz_mat[...] = jnp.where(iota((384, 256), 1) == target, 1.0, 0.0).astype(jnp.bfloat16)
+    place = iota((128, 384), 1) - 24 * gz
+    halves[...] = jnp.where((place & 1) == iota((128, 384), 0) // 64, 1.0 / 16.0, 0.0).astype(jnp.bfloat16)
+    place = iota((48, 384), 1) - 24 * gz
+    row48 = iota((48, 384), 0)
+    keep = (place >= 0) & (place < 24) & ((place // 4) == (row48 // 8))
+    keep = keep & ((row48 % 8) // 2 == (place // 2) % 2) & (row48 % 8 < 4)
+    keep48[...] = jnp.where(keep, 1.0, 0.0)
 
     col = iota((128, 256), 0)
     quarter = iota((128, 256), 1) // 64
     code = 2 * (col // 24) + (col % 2)
-    sel[...] = jnp.where(code == jnp.where(quarter == 3, 1, quarter + 2), 1.0, 0.0)
+    sel[...] = jnp.where(code == jnp.where(quarter == 3, 1, quarter + 2), 1.0, 0.0).astype(jnp.bfloat16)
 
     for copy in round_z:
         copy.wait_recv()
@@ -255,27 +277,38 @@
         cen[x] = 0.9 * mid + wide
         dinv[x] = inverse
 
-    for copy in round_r:
+    def begin(start, stop):
+        @pl.loop(start, stop, unroll=4)
+        def _(x):
+            for c in range(3):
+                s_a[c, x] = dinv[x] * res[c, x]
+
+    for copy in round_y:
         copy.wait_recv()
-
-    @pl.loop(0, 16, unroll=4)
-    def _(x):
-        for c in range(3):
-            s_a[c, x] = dinv[x] * res[c, x]
+    begin(4, 12)
 
     def fine(ref):
         return functools.partial(
             operate, lambda c, x: ref[c, x], lambda x: e16[x], lambda x: cen[x]
         )
 
-    def sweep(source, out, start, stop):
-        @pl.loop(start, stop, unroll=UNROLL)
-        def _(x):
-            image = fine(source)(x)
-            for c in range(3):
-                out[c, x] = source[c, x] + dinv[x] * (res[c, x] - image[c])
-
-    sweep(s_a, s_b, 1, 15)
+    def sweep(source, out, start, stop, count=STEP):
+        assert (stop - start) % count == 0
+
+        @pl.loop(0, (stop - start) // count, unroll=UNROLL)
+        def _(k):
+            x = start + count * k
+            for i, image in enumerate(fine(source)(x, count)):
+                for c in range(3):
+                    out[c, x + i] = source[c, x + i] + dinv[x + i] * (res[c, x + i] - image[c])
+
+    sweep(s_a, s_b, 5, 11, 2)
+    for copy in round_r:
+        copy.wait_recv()
+    begin(0, 4)
+    begin(12, 16)
+    sweep(s_a, s_b, 1, 5, 2)
+    sweep(s_a, s_b, 11, 15, 2)
 
     def put_tiles(ref, f, k, value):
         for t in range(3):
@@ -284,7 +317,7 @@
     @pl.loop(0, 6)
     def _(k):
         x = 2 * k + 2
-        first, second = fine(s_b)(x), fine(s_b)(x + 1)
+        first, second = fine(s_b)(x, 2)
         for c in range(3):
             both = (res[c, x] - first[c]) + (res[c, x + 1] - second[c])
             put_tiles(ysum, c, k + 1, both + pltpu.roll(both, 15, 0))
@@ -321,19 +354,13 @@
         apply = functools.partial(
             operate, lambda c, k: m_a[c, k], lambda k: km[3, k], lambda k: cen1[k]
         )
-        first, second = apply(x), apply(x + 1)
+        first, second = apply(x, 2)
         for c in range(3):
             both = (km[c, x] - first[c]) + (km[c, x + 1] - second[c])
             tlow[2 * c + b] = both[:, 0:128]
 
-    place = iota((128, 384), 1) - 24 * gz
-    halves = jnp.where((place & 1) == iota((128, 384), 0) // 64, 1.0 / 16.0, 0.0)
-    spread = dot(tlow[...].reshape(48, 128), halves)
-    place = iota((48, 384), 1) - 24 * gz
-    row48 = iota((48, 384), 0)
-    keep = (place >= 0) & (place < 24) & ((place // 4) == (row48 // 8))
-    keep = keep & ((row48 % 8) // 2 == (place // 2) % 2) & (row48 % 8 < 4)
-    own_g = jnp.sum(jnp.where(keep, spread, 0.0), axis=0, keepdims=True)
+    spread = dot(tlow[...].reshape(48, 128), halves[...])
+    own_g = jnp.sum(jnp.where(keep48[...] > 0.0, spread, 0.0), axis=0, keepdims=True)
     gsend[...] = own_g
     round_b = [send(gsend, grecv.at[k], d) for k, d in enumerate(column)]
 
@@ -441,17 +468,16 @@
                         m_b[c, x, 0:8] += upper_tile
                         m_b[c, x, 8:16] += lower_tile
 
-    @pl.loop(2, 10, unroll=UNROLL)
-    def _(x):
-        image = operate(lambda c, k: m_b[c, k], lambda k: wd[3, k], lambda k: cenw[k], x)
-        for c in range(3):
-            value = m_b[c, x] + dinvw[x] * (wd[c, x] - image[c])
-            u8[c, x - 2] = jnp.where(row_in_8 < 6, value[0:8], value[8:16])
-
-    fine_u = lax.dot_general(
-        u8[...].reshape(192, 256), rz_mat[...], (((1,), (1,)), ((), ())),
-        precision=HIGH, preferred_element_type=F32,
-    ).reshape(3, 8, 8, 384)
+    @pl.loop(0, 4)
+    def _(k):
+        x = 2 * k + 2
+        images = operate(lambda c, k: m_b[c, k], lambda k: wd[3, k], lambda k: cenw[k], x, 2)
+        for i, image in enumerate(images):
+            for c in range(3):
+                value = m_b[c, x + i] + dinvw[x + i] * (wd[c, x + i] - image[c])
+                u8[c, x + i - 2] = jnp.where(row_in_8 < 6, value[0:8], value[8:16])
+
+    fine_u = dot(u8[...].reshape(192, 256), rz_mat[...], (((1,), (1,)), ((), ()))).reshape(3, 8, 8, 384)
     for t in range(3):
         piece = fine_u[:, :, :, 128 * t : 128 * t + 128]
         ysum[0:3, :, t, pl.ds(0, 8, stride=2), :] = piece
@@ -468,18 +494,19 @@
     sweep(s_a, s_b, 2, 14)
     sweep(s_b, s_a, 3, 13)
 
-    def last(x, sums):
-        image = fine(s_a)(x + 4)
+    def last(k, sums):
         new = list(sums)
-        for c in range(3):
-            p = s_a[c, x + 4, 0:8, 0:256]
-            ap = image[c][0:8, 0:256]
-            d = pdir[c, x]
-            q = pimg[c, x]
-            p_out[c, x] = p
-            ap_out[c, x] = ap
-            terms = (res[c, x + 4, 0:8, 0:256] * p, p * ap, p * q + d * ap, d * q)
-            new = [a + b for a, b in zip(new, terms)]
+        for i, image in enumerate(fine(s_a)(2 * k + 4, 2)):
+            x = 2 * k + i
+            for c in range(3):
+                p = s_a[c, x + 4, 0:8, 0:256]
+                ap = image[c][0:8, 0:256]
+                d = pdir[c, x]
+                q = pimg[c, x]
+                p_out[c, x] = p
+                ap_out[c, x] = ap
+                terms = (res[c, x + 4, 0:8, 0:256] * p, p * ap, p * q + d * ap, d * q)
+                new = [a + b for a, b in zip(new, terms)]
         return tuple(new)
 
     zero = jnp.zeros((8, 256), F32)
@@ -487,7 +514,7 @@
         pltpu.make_async_copy(p_out, p_hbm, lsem.at[0]),
         pltpu.make_async_copy(ap_out, ap_hbm, lsem.at[1]),
     ]
-    sums = lax.fori_loop(0, 8, last, (zero, zero, zero, zero), unroll=UNROLL)
+    sums = lax.fori_loop(0, 4, last, (zero, zero, zero, zero))
     group = iota((1, 128), 1) // 32
     mine = jnp.zeros((1, 128), F32)
     for i, value in enumerate(sums):
@@ -580,7 +607,8 @@
             vm(2, 8, 128), vm(2, 3, 3, 8, 128),
             vm(4, 12, 16, 256), vm(12, 16, 256), vm(12, 16, 256),
             vm(3, 12, 16, 256), vm(8, 128), vm(3, 8, 8, 256),
-            vm(384, 256), vm(128, 256),
+            pltpu.VMEM((384, 256), jnp.bfloat16), pltpu.VMEM((128, 256), jnp.bfloat16),
+            pltpu.VMEM((128, kc), jnp.bfloat16), vm(48, kc),
             vm(1, kc), vm(n_col, 1, kc), vm(128, kc),
             vm(1, 128), vm(3, 3, 1, 128),
             vm(1, 128), vm(n_layer, 1, 128), vm(1, 128), vm(n_col, 1, 128),

time: 56.7 us -> 55.3 us (0.975)
  Pallas kernels: 55.2 us -> 53.8 us
    pallas_call x1, Pallas kernels: 52.9 us -> 51.5 us  [on_device(): pl.pallas_call(functools.partial(kernel, ng), name='cg_step', out_shape=(...]
where the time goes in v3:
time: 55.3 us; the launch traced here: 55.1 us
  Pallas kernels  53.8 us (97%)
  between operations  1.28 us (2%)
    pallas_call x1, Pallas kernels, on_device(): pl.pallas_call(functools.partial(kernel, ng), name='cg_step', out_shape=(...  51.5 us
    pallas_call x1, Pallas kernels, on_device(): pl.pallas_call(finish, name='cg_finish', out_shape=(field,) * 4, in_specs...  2.31 us

profile of v3, /device:TPU:1, one launch (start us, length us, event | category | flops | bytes accessed | tf_op | source)
XLA Modules:
  0.0 55.1 jit_solution(109608527155345154)
XLA Ops:
  1.3 51.5 %cg_step.1 = (f32[3,8,8,256]{3,2,1,0:T(8,128)}, f32[3,8,8,256]{3,2,1,0:T(8,128)}, f32[1,128]{1,0:T(1,128)}) custom-call(f32[3,8,8,256]{3,2,1,0:T(8,128)} %refs_3_.1, f32[3,8,8,256]{3,2,1,0:T(8,128)} %refs_0_.1, f32[3,8,8,256]{3,2,1,0:T(8,128)} %refs_1_.1, s32[8,8,256]{2,1,0:T(8,128)} %dens_hbm.1, f32[1,1,384,384]{3,2,1,0:T(8,128)} %inv_hbm.1, f32[16]{0:T(128)} %table_hbm.1, ...), custom_call_target="tpu_custom_call" | custom-call | tf_op jit(solution)/shard_map/cg_step/pallas_call | solution.py:624
  52.8 2.3 %cg_finish.1 = (f32[3,8,8,256]{3,2,1,0:T(8,128)}, f32[3,8,8,256]{3,2,1,0:T(8,128)}, f32[3,8,8,256]{3,2,1,0:T(8,128)}, f32[3,8,8,256]{3,2,1,0:T(8,128)}) custom-call(f32[3,8,8,256]{3,2,1,0:T(8,128)} %refs_0_.1, f32[3,8,8,256]{3,2,1,0:T(8,128)} %refs_1_.1, f32[3,8,8,256]{3,2,1,0:T(8,128)} %refs_2_.1, f32[3,8,8,256]{3,2,1,0:T(8,128)} %refs_3_.1, ...), custom_call_target="tpu_custom_call" | custom-call | tf_op jit(solution)/shard_map/cg_finish/pallas_call | solution.py:635

commit v4 on v3

--- a/solution.py
+++ b/solution.py
@@ -100,7 +100,7 @@
     layer = [(i, j, 0) for i in range(ng[0]) for j in range(ng[1]) if (i, j) != (0, 0)]
     layer.sort(key=hops, reverse=True)
     partners = []
-    for d in near + column + layer:
+    for d in sorted(near + column + layer, key=hops, reverse=True):
         d = tuple(d[i] % ng[i] for i in range(3))
         if d not in partners:
             partners.append(d)
@@ -523,12 +523,19 @@
         value = value + pltpu.roll(value, 32, 1)
         mine = jnp.where(group == i, value, mine)
 
+    pending = list(started)
     for peers, out, into in ((layer, dsend, drecv), (column, esend, erecv)):
         out[...] = mine
         copies = [send(out, into.at[k], d) for k, d in enumerate(peers)]
         if peers is layer:
             for copy in stores:
                 copy.start()
+        else:
+            for copy in stores:
+                copy.wait()
+        for copy in pending:
+            copy.wait_send()
+        pending = copies
         for copy in copies:
             copy.wait_recv()
         for k in range(len(peers)):
@@ -539,9 +546,7 @@
     beta = inner_rz / prev_rz[0]
     alpha = inner_rz / (pp + beta * (cross + beta * qq))
     ab_out[...] = jnp.where(group < 2, alpha, beta)
-    for copy in stores:
-        copy.wait()
-    for copy in started:
+    for copy in pending:
         copy.wait_send()
 
 

time: 55.3 us -> 54.9 us (level)
  no operation moved by 1% of the time
where the time goes in v4:
time: 54.9 us; the launch traced here: 54.7 us
  Pallas kernels  53.4 us (97%)
  between operations  1.28 us (2%)
    pallas_call x1, Pallas kernels, on_device(): pl.pallas_call(functools.partial(kernel, ng), name='cg_step', out_shape=(...  51.1 us
    pallas_call x1, Pallas kernels, on_device(): pl.pallas_call(finish, name='cg_finish', out_shape=(field,) * 4, in_specs...  2.31 us

profile of v4, /device:TPU:1, one launch (start us, length us, event | category | flops | bytes accessed | tf_op | source)
XLA Modules:
  0.0 54.7 jit_solution(14045300088409061575)
XLA Ops:
  1.3 51.1 %cg_step.1 = (f32[3,8,8,256]{3,2,1,0:T(8,128)}, f32[3,8,8,256]{3,2,1,0:T(8,128)}, f32[1,128]{1,0:T(1,128)}) custom-call(f32[3,8,8,256]{3,2,1,0:T(8,128)} %refs_3_.1, f32[3,8,8,256]{3,2,1,0:T(8,128)} %refs_0_.1, f32[3,8,8,256]{3,2,1,0:T(8,128)} %refs_1_.1, s32[8,8,256]{2,1,0:T(8,128)} %dens_hbm.1, f32[1,1,384,384]{3,2,1,0:T(8,128)} %inv_hbm.1, f32[16]{0:T(128)} %table_hbm.1, ...), custom_call_target="tpu_custom_call" | custom-call | tf_op jit(solution)/shard_map/cg_step/pallas_call | solution.py:629
  52.4 2.3 %cg_finish.1 = (f32[3,8,8,256]{3,2,1,0:T(8,128)}, f32[3,8,8,256]{3,2,1,0:T(8,128)}, f32[3,8,8,256]{3,2,1,0:T(8,128)}, f32[3,8,8,256]{3,2,1,0:T(8,128)}) custom-call(f32[3,8,8,256]{3,2,1,0:T(8,128)} %refs_0_.1, f32[3,8,8,256]{3,2,1,0:T(8,128)} %refs_1_.1, f32[3,8,8,256]{3,2,1,0:T(8,128)} %refs_2_.1, f32[3,8,8,256]{3,2,1,0:T(8,128)} %refs_3_.1, ...), custom_call_target="tpu_custom_call" | custom-call | tf_op jit(solution)/shard_map/cg_finish/pallas_call | solution.py:640

commit v5 on v4

--- a/solution.py
+++ b/solution.py
@@ -17,6 +17,7 @@
 DAMP = 0.6
 UNROLL = 2
 STEP = 2
+HELD = 300
 EIGHTIETH = 0.0125
 SMALL = (-1, 0, 1)
 
@@ -75,12 +76,12 @@
 def kernel(
     ng,
     res_hbm, dir_hbm, img_hbm, dens_hbm, inv_hbm, table_hbm, rz_hbm,
-    p_hbm, ap_hbm, ab_out,
+    held_hbm,
     dens, res, ewide, e16, cen, dinv, s_a, s_b, pdir, pimg,
     spack, srecv, ysum, km, cen1, dinv1, m_a, tlow,
     mpack, mrecv, wd, cenw, dinvw, m_b, m_c, u8,
     rz_mat, sel, halves, keep48, gsend, grecv, rows, wsend, wrecv,
-    dsend, drecv, esend, erecv, p_out, ap_out, table, prev_rz,
+    dsend, drecv, esend, erecv, p_out, ap_out, ab_out, table, prev_rz,
     lsem, sems, recs,
 ):
     gx, gy, gz = (lax.axis_index(a) for a in AXES)
@@ -188,7 +189,7 @@
     }
     main = slice(0, 256)
     round_z, round_e, round_y, round_r = [], [], [], []
-    for d in tilted:
+    for d in tilted[::-1]:
         side = 0 if d[2] < 0 else 1
         round_z.append(send(spack.at[side], srecv.at[side, 1 - d[0], 1 - d[1]], d))
     for d in flat:
@@ -389,9 +390,7 @@
         copy.wait()
     for copy in round_b:
         copy.wait_recv()
-    g = own_g
-    for k in range(len(column)):
-        g = g + grecv[k]
+    g = own_g + jnp.sum(grecv[...], axis=0)
     g = jnp.broadcast_to(g, (8, g.shape[1]))
     w = lax.dot_general(
         g, rows[...], (((1,), (1,)), ((), ())), precision=HIGH, preferred_element_type=F32
@@ -491,8 +490,8 @@
                 lanes = slice(128 * t, 128 * t + 128)
                 s_a[c, x, :, lanes] = s_b[c, x, :, lanes] + ysum[c, k, t]
 
-    sweep(s_a, s_b, 2, 14)
-    sweep(s_b, s_a, 3, 13)
+    sweep(s_a, s_b, 2, 14, 3)
+    sweep(s_b, s_a, 3, 13, 5)
 
     def last(k, sums):
         new = list(sums)
@@ -511,8 +510,8 @@
 
     zero = jnp.zeros((8, 256), F32)
     stores = [
-        pltpu.make_async_copy(p_out, p_hbm, lsem.at[0]),
-        pltpu.make_async_copy(ap_out, ap_hbm, lsem.at[1]),
+        pltpu.make_async_copy(p_out, held_hbm.at[0], lsem.at[0]),
+        pltpu.make_async_copy(ap_out, held_hbm.at[1], lsem.at[1]),
     ]
     sums = lax.fori_loop(0, 4, last, (zero, zero, zero, zero))
     group = iota((1, 128), 1) // 32
@@ -538,33 +537,29 @@
         pending = copies
         for copy in copies:
             copy.wait_recv()
-        for k in range(len(peers)):
-            mine = mine + into[k]
+        mine = mine + jnp.sum(into[...], axis=0)
     inner_rz, pp, cross, qq = (
         jnp.sum(jnp.where(group == i, mine, 0.0), axis=1, keepdims=True) for i in range(4)
     )
     beta = inner_rz / prev_rz[0]
     alpha = inner_rz / (pp + beta * (cross + beta * qq))
-    ab_out[...] = jnp.where(group < 2, alpha, beta)
+    ab_out[...] = jnp.broadcast_to(jnp.where(group < 2, alpha, beta), (8, 128))
+    last_store = pltpu.make_async_copy(ab_out, held_hbm.at[2, 0, 0, :, 0:128], lsem.at[2])
+    last_store.start()
+    last_store.wait()
     for copy in pending:
         copy.wait_send()
 
 
-def finish(
-    *refs,
-):
-    sources, ab_hbm, targets = refs[0:6], refs[6], refs[7:11]
-    held, ab, made, sems, outs = refs[11:17], refs[17], refs[18:22], refs[22], refs[23]
-    ab_load = pltpu.make_async_copy(ab_hbm, ab, sems.at[3, 0])
+def finish(pdir, pimg, sol, res, held_hbm, *refs):
+    targets, held, ab, made, sems, outs = refs[0:4], refs[4], refs[5], refs[6:10], refs[10], refs[11]
+    ab_load = pltpu.make_async_copy(held_hbm.at[2, 0, 0, :, 0:128], ab, sems.at[3, 0])
     ab_load.start()
-    loads = [
-        [pltpu.make_async_copy(src.at[c], dst.at[c], sems.at[c, i]) for i, (src, dst) in enumerate(zip(sources, held))]
-        for c in range(3)
-    ]
+    loads = [[pltpu.make_async_copy(held_hbm.at[i, c], held.at[i, c], sems.at[c, i]) for i in range(2)] for c in range(3)]
     for part in loads:
         for copy in part:
             copy.start()
-    pdir, pimg, sol, res, p, ap = held
+    p, ap = held.at[0], held.at[1]
     new_sol, new_res, new_dir, new_img = made
     ab_load.wait()
     alpha = jnp.broadcast_to(ab[0:1, 0:1], (8, 256))
@@ -617,7 +612,7 @@
             vm(1, kc), vm(n_col, 1, kc), vm(128, kc),
             vm(1, 128), vm(3, 3, 1, 128),
             vm(1, 128), vm(n_layer, 1, 128), vm(1, 128), vm(n_col, 1, 128),
-            vm(3, 8, 8, 256), vm(3, 8, 8, 256),
+            vm(3, 8, 8, 256), vm(3, 8, 8, 256), vm(8, 128),
             pltpu.SMEM(table.shape, F32), pltpu.SMEM((1,), F32),
             pltpu.SemaphoreType.DMA((9,)),
             pltpu.SemaphoreType.DMA((copies,)),
@@ -626,12 +621,12 @@
         in_hbm = pl.BlockSpec(memory_space=pltpu.HBM)
         in_vmem = pl.BlockSpec(memory_space=pltpu.VMEM)
         field = jax.ShapeDtypeStruct(res.shape, F32)
-        p, ap, ab = pl.pallas_call(
+        held = pl.pallas_call(
             functools.partial(kernel, ng),
             name="cg_step",
-            out_shape=(field, field, jax.ShapeDtypeStruct((1, 128), F32)),
+            out_shape=jax.ShapeDtypeStruct((HELD,) + res.shape, F32),
             in_specs=[in_hbm] * 7,
-            out_specs=(in_hbm, in_hbm, in_vmem),
+            out_specs=in_hbm,
             scratch_shapes=scratch,
             compiler_params=pltpu.CompilerParams(
                 collective_id=0, has_side_effects=True, vmem_limit_bytes=56 << 20
@@ -641,12 +636,12 @@
             finish,
             name="cg_finish",
             out_shape=(field,) * 4,
-            in_specs=[in_hbm] * 7,
+            in_specs=[in_vmem] * 4 + [in_hbm],
             out_specs=(in_hbm,) * 4,
-            scratch_shapes=[vm(*res.shape)] * 6 + [vm(1, 128)] + [vm(*res.shape)] * 4
-            + [pltpu.SemaphoreType.DMA((4, 6)), pltpu.SemaphoreType.DMA((3, 4))],
-            compiler_params=pltpu.CompilerParams(vmem_limit_bytes=56 << 20),
-        )(pdir, pimg, sol, res, p, ap, ab)
+            scratch_shapes=[vm(2, *res.shape), vm(8, 128)] + [vm(*res.shape)] * 4
+            + [pltpu.SemaphoreType.DMA((4, 2)), pltpu.SemaphoreType.DMA((3, 4))],
+            compiler_params=pltpu.CompilerParams(vmem_limit_bytes=16 << 20),
+        )(pdir, pimg, sol, res, held)
 
     split = P(None, *AXES)
     return jax.shard_map(

time: 54.9 us -> 54.5 us (level)
  no operation moved by 1% of the time
where the time goes in v5:
time: 54.5 us; the launch traced here: 54.4 us
  Pallas kernels  52.9 us (97%)
  between operations  1.42 us (3%)
    pallas_call x1, Pallas kernels, on_device(): pl.pallas_call(functools.partial(kernel, ng), name='cg_step', out_shape=j...  51 us
    pallas_call x1, Pallas kernels, on_device(): pl.pallas_call(finish, name='cg_finish', out_shape=(field,) * 4, in_specs...  1.93 us

profile of v5, /device:TPU:1, one launch (start us, length us, event | category | flops | bytes accessed | tf_op | source)
XLA Modules:
  0.0 54.4 jit_solution(14272343672195503642)
XLA Ops:
  0.6 0.0 copy-start.1
  0.6 0.0 copy-start
  0.7 0.0 copy-start.2
  0.7 0.0 copy-start.3
  1.4 51.0 %cg_step.1.held_hbm = f32[300,3,8,8,256]{4,3,2,1,0:T(8,128)} custom-call(f32[3,8,8,256]{3,2,1,0:T(8,128)} %res.1, f32[3,8,8,256]{3,2,1,0:T(8,128)} %pdir.1, f32[3,8,8,256]{3,2,1,0:T(8,128)} %pimg.1, s32[8,8,256]{2,1,0:T(8,128)} %dens_hbm.1, f32[1,1,384,384]{3,2,1,0:T(8,128)} %inv_hbm.1, f32[16]{0:T(128)} %table_hbm.1, f32[1]{0:T(128)} %bitcast.1.rz_hbm), custom_call_target="tpu_custom_call" | custom-call | tf_op jit(solution)/shard_map/cg_step/pallas_call | solution.py:624
  52.4 0.0 copy-done.1
  52.4 0.0 copy-done
  52.4 0.0 copy-done.2
  52.4 0.0 copy-done.3
  52.4 1.9 %cg_finish.1 = (f32[3,8,8,256]{3,2,1,0:T(8,128)}, f32[3,8,8,256]{3,2,1,0:T(8,128)}, f32[3,8,8,256]{3,2,1,0:T(8,128)}, f32[3,8,8,256]{3,2,1,0:T(8,128)}) custom-call(f32[3,8,8,256]{3,2,1,0:T(8,128)S(1)} %copy-done, f32[3,8,8,256]{3,2,1,0:T(8,128)S(1)} %copy-done.1, f32[3,8,8,256]{3,2,1,0:T(8,128)S(1)} %copy-done.3, f32[3,8,8,256]{3,2,1,0:T(8,128)S(1)} %copy-done.2, ...), custom_call_target="tpu_custom_call" | custom-call | tf_op jit(solution)/shard_map/cg_finish/pallas_call | solution.py:635
Async XLA Ops:
  0.6 51.8 %copy-start.1 = (f32[3,8,8,256]{3,2,1,0:T(8,128)S(1)}, f32[3,8,8,256]{3,2,1,0:T(8,128)}, u32[]{:S(2)}) copy-start(f32[3,8,8,256]{3,2,1,0:T(8,128)} %pimg.1) | copy-start | bytes 589828
  0.6 51.8 %copy-start = (f32[3,8,8,256]{3,2,1,0:T(8,128)S(1)}, f32[3,8,8,256]{3,2,1,0:T(8,128)}, u32[]{:S(2)}) copy-start(f32[3,8,8,256]{3,2,1,0:T(8,128)} %pdir.1) | copy-start | bytes 589828
  0.7 51.8 %copy-start.2 = (f32[3,8,8,256]{3,2,1,0:T(8,128)S(1)}, f32[3,8,8,256]{3,2,1,0:T(8,128)}, u32[]{:S(2)}) copy-start(f32[3,8,8,256]{3,2,1,0:T(8,128)} %res.1) | copy-start | bytes 589828
  0.7 51.8 %copy-start.3 = (f32[3,8,8,256]{3,2,1,0:T(8,128)S(1)}, f32[3,8,8,256]{3,2,1,0:T(8,128)}, u32[]{:S(2)}) copy-start(f32[3,8,8,256]{3,2,1,0:T(8,128)} %sol.1) | copy-start | bytes 589828
